TPU v7x, 512 devices: a whole 4x8x8 slice. The times are simulated.
512 devices in a mesh: tile: 64 (over y, x, core), view: 8 (over z).
Axes of the slice: x: 4, y: 8, z: 8, core: 2. Of those that a mesh axis runs over, the one named last changes fastest.
Arguments:
- volume: float32 [64, 512, 512], P(None, 'tile'), may hold values from 0.09 to 7.2
- weights: bfloat16 [64, 32, 32, 48, 256], P('tile', 'view'), may hold values from 0 to 0.0546875
- measured: float32 [64, 8, 1, 64, 48], P('tile', 'view'), may hold values from 4 to 40
- crossings: int32 [64, 32, 32, 2], P('tile', 'view'), may hold values from 0 to 15, as said below
- counts: int32 [64, 32], P('tile', 'view'), may hold values from 16 to 32
Outputs:
- updated: float32 [64, 512, 512], P(None, 'tile')
Inputs may be any that keep to these rules, and one draw needn't show every extreme that they name: `crossings`: slots follow a parallel-beam geometry: each segment of a strip has one or two live slots, naming the one or two adjacent blocks that its pixels' footprints reach in that view; the live slots of a strip and view come first; a dead slot repeats the first block of its segment.
All inputs are finite; a program needn't handle non-finite values.
Results may differ from a plain program's by a relative error of at most 0.002.
Values may be sent and summed in bfloat16 or wider, within the bound.
A program may use at most 64 MiB of HBM per device.

v0:
```python
import jax
import jax.numpy as jnp
from jax import lax
from jax.sharding import PartitionSpec as P

BACKGROUND = 1.0
HUBER_DELTA = 0.1


def extended(x, sides, width):
    for axis, dim in sides:
        peers, length = (lax.axis_size(axis), x.shape[dim])
        up = [(i, (i + 1) % peers) for i in range(peers - 1)]
        down = [(j, i) for i, j in up]
        last = lax.slice_in_dim(x, length - width, length, axis=dim)
        initial = lax.slice_in_dim(x, 0, width, axis=dim)
        before = lax.ppermute(last, axis, up)
        after = lax.ppermute(initial, axis, down)
        x = jnp.concatenate([before, x, after], axis=dim)
    return x


def per_device(volume, weights, measured, crossings, counts):
    high = lax.Precision.HIGHEST
    tile_count = lax.axis_size("tile")
    view_local = weights.shape[1]
    slot_count = weights.shape[2]
    bin_count = weights.shape[3]
    seg_pixels = weights.shape[4]
    plane_count = volume.shape[0]
    row_count = volume.shape[1]
    col_count = volume.shape[2]
    seg_cols = seg_pixels // row_count
    seg_total = col_count // seg_cols
    owned = measured.shape[2]
    blocks_view = owned * tile_count // view_local
    block_total = tile_count * owned
    slot_total = view_local * slot_count
    flat_width = plane_count * bin_count
    slot_weights = weights.reshape(slot_total, bin_count, seg_pixels)
    block_of = crossings[0, :, :, 0].reshape(slot_total)
    segment_of = crossings[0, :, :, 1].reshape(slot_total)
    alive = (jnp.arange(slot_count, dtype=jnp.int32)[None, :] < counts[0][:, None]).reshape(
        slot_total
    )
    alive_f = alive.astype(jnp.float32)
    view_slot = jnp.arange(slot_total, dtype=jnp.int32) // slot_count
    global_block = view_slot * blocks_view + block_of
    block_onehot = (
        global_block[:, None] == jnp.arange(block_total, dtype=jnp.int32)[None, :]
    ).astype(jnp.float32)
    block_onehot = block_onehot * alive_f[:, None]
    segment_onehot = (
        segment_of[:, None] == jnp.arange(seg_total, dtype=jnp.int32)[None, :]
    ).astype(jnp.float32)
    segments = volume.astype(jnp.bfloat16).reshape(plane_count, row_count, seg_total, seg_cols)
    segments = segments.transpose(0, 2, 1, 3).reshape(plane_count, seg_total, seg_pixels)
    slot_volume = jnp.einsum(
        "sq,pqx->spx",
        segment_onehot.astype(jnp.bfloat16),
        segments,
        preferred_element_type=jnp.float32,
    ).astype(jnp.bfloat16)
    partial_value = jnp.einsum(
        "spx,snx->spn", slot_volume, slot_weights, preferred_element_type=jnp.float32
    )
    dense = jnp.dot(block_onehot.T, partial_value.reshape(slot_total, flat_width), precision=high)
    dense = dense.reshape(tile_count, owned, flat_width)
    projection = lax.psum_scatter(dense, "tile", scatter_dimension=0, tiled=True)[0]
    ratios = (measured[0, 0].reshape(owned, flat_width) / (projection + BACKGROUND)).astype(
        jnp.bfloat16
    )
    every_block = lax.all_gather(ratios, "tile", axis=0, tiled=True)
    picked = jnp.dot(
        block_onehot.astype(jnp.bfloat16), every_block, preferred_element_type=jnp.float32
    ).astype(jnp.bfloat16)
    picked = picked.reshape(slot_total, plane_count, bin_count)
    spread_back = jnp.einsum(
        "spn,snx->spx", picked, slot_weights, preferred_element_type=jnp.float32
    )
    back_sum = jnp.einsum("sq,spx->pqx", segment_onehot, spread_back, precision=high)
    back_sum = back_sum.reshape(plane_count, seg_total, row_count, seg_cols).transpose(0, 2, 1, 3)
    back_sum = back_sum.reshape(volume.shape)
    live_segments = (segment_onehot * alive_f[:, None]).astype(jnp.bfloat16)
    sensitivity = jnp.einsum(
        "sq,snx->qx", live_segments, slot_weights, preferred_element_type=jnp.float32
    )
    sensitivity = (
        sensitivity.reshape(seg_total, row_count, seg_cols)
        .transpose(1, 0, 2)
        .reshape(row_count, col_count)
    )
    widened = extended(volume, (("tile", 1),), 1)
    padded = jnp.pad(widened, ((1, 1), (0, 0), (1, 1)))
    centre = padded[1:-1, 1:-1, 1:-1]
    penalty = jnp.zeros_like(volume)
    for other in (
        padded[2:, 1:-1, 1:-1],
        padded[:-2, 1:-1, 1:-1],
        padded[1:-1, 2:, 1:-1],
        padded[1:-1, :-2, 1:-1],
        padded[1:-1, 1:-1, 2:],
        padded[1:-1, 1:-1, :-2],
    ):
        penalty = penalty + jnp.clip(centre - other, -HUBER_DELTA, HUBER_DELTA)
    back_total, sens_total = lax.psum((back_sum, sensitivity), "view")
    return volume * back_total / (sens_total[None] * (1.0 + penalty))


def solution(mesh):
    in_specs = (
        P(None, "tile", None),
        P("tile", "view", None, None, None),
        P("tile", "view", None, None, None),
        P("tile", "view", None, None),
        P("tile", "view"),
    )
    out_specs = P(None, "tile", None)
    return jax.shard_map(
        per_device, mesh=mesh, in_specs=in_specs, out_specs=out_specs, check_vma=False
    )
```

profile of v0, /device:TPU:6, one launch (start us, length us, event | category | flops | bytes accessed | tf_op | source)
XLA Modules:
  0.0 397.5 jit_solution(3167328225006800716)
XLA Ops:
  6.5 0.8 slice_reduce_fusion.1
  7.4 1.8 copy.79
  9.2 0.1 copy.80
  9.3 1.6 copy.81
  11.0 2.5 convolution_convert_fusion.1
  13.4 4.5 %fusion.2 = f32[128,64,48]{1,2,0:T(8,128)} fusion(bf16[128,48,256]{2,1,0:T(8,128)(2,1)S(1)} %bitcast.51, bf16[128,64,256]{2,0,1:T(8,128)(2,1)S(1)} %convolution_convert_fusion.1), kind=kOutput, calls=%fused_computation.3 | convolution fusion | flops 201326592 | bytes 8912896 | tf_op jit(solution)/shard_map/spx,snx->spn/dot_general | solution.py:64
  17.9 3.3 copy.83
  21.4 4.1 %convolution_bitcast_fusion = f32[64,1,3072]{2,0,1:T(8,128)} fusion(f32[128,3072]{0,1:T(8,128)} %bitcast.55, f32[128]{0:T(128)S(1)} %reshape.107, s32[128]{0:T(128)S(1)} %fusion.50), kind=kOutput, calls=%fused_computation.10 | convolution fusion | flops 302006272 | bytes 2360320 | tf_op jit(solution)/shard_map/dot_general | solution.py:67
  25.7 0.1 reshape_squeeze.7
  25.8 1.3 dynamic-slice
  27.2 198.3 %all-reduce.7.cloned.1.call-done = f32[64,1,3072]{2,0,1:T(8,128)} async-done(((f32[64,1,3072]{2,0,1:T(8,128)}), f32[64,1,3072]{2,0,1:T(8,128)}) %all-reduce.7.cloned.1.call-update) | async-done | bytes 786448
  225.4 1.6 convert_bitcast_fusion
  227.0 48.9 %all-gather = bf16[64,1,3072]{2,1,0:T(2,128)(2,1)S(1)} all-gather(bf16[1,1,3072]{2,1,0:T(2,128)(2,1)S(1)} %convert_bitcast_fusion), channel_id=1, replica_groups=mesh['tile'=64,'view'=8] {'tile'}, dimensions={0}, use_global_device_ids=true | all-gather | bytes 399360 | tf_op jit(solution)/shard_map/all_gather | solution.py:73
  275.8 1.3 convolution_convert_fusion
  277.1 2.3 copy.84
  279.4 3.1 copy.85
  282.5 2.7 fusion.55
  285.2 8.5 %fusion.7 = f32[64,16,256]{2,1,0:T(8,128)} fusion(f32[128,64,256]{2,1,0:T(8,128)S(1)} %fusion.55, s32[128]{0:T(128)S(1)} %eq.31), kind=kOutput, calls=%fused_computation.17 | convolution fusion | flops 402655232 | bytes 9437696 | tf_op jit(solution)/shard_map/sq,spx->pqx/dot_general | solution.py:81
  293.7 3.2 copy.87
  296.9 3.1 copy.88
  300.1 3.4 copy.89
  303.4 2.5 fusion.54
  305.9 2.2 collective-permute-start
  308.2 3.5 collective-permute-start.1
  311.7 0.9 convert_reduce_fusion
  312.6 0.1 copy.90
  312.7 0.2 convolution_bitcast_fusion.1
  312.9 0.1 reshape.106
  313.0 30.8 %psum.15 = f32[8,512]{1,0:T(8,128)S(1)} all-reduce(f32[8,512]{1,0:T(8,128)S(1)} %reshape.106), channel_id=1, replica_groups=mesh['tile'=64,'view'=8] {'view'}, use_global_device_ids=true, to_apply=%region_3.4 | all-reduce | flops 4096 | bytes 32768 | tf_op jit(solution)/shard_map/psum | solution.py:106
  343.9 3.0 select_maximum_fusion
  346.9 39.3 %all-reduce.5.cloned.1.call-done = f32[64,8,512]{2,1,0:T(8,128)} async-done(((f32[64,8,512]{2,1,0:T(8,128)}), f32[64,8,512]{2,1,0:T(8,128)}) %all-reduce.5.cloned.1.call-update) | async-done | bytes 1048592 | tf_op jit(solution)/shard_map/psum | solution.py:106
  386.2 4.5 %fusion.14 = f32[64,8,512]{2,1,0:T(8,128)} fusion(f32[64,8,512]{2,1,0:T(8,128)} %param.5, f32[66,10,514]{2,1,0:T(8,128)S(1)} %select_maximum_fusion, f32[64,1,512]{2,1,0:T(1,128)S(1)} %collective-permute-done, f32[64,1,512]{2,1,0:T(1,128)S(1)} %collective-permute-done.1, f32[64,8,512]{2,1,0:T(8,128)} %all-reduce.5.cloned.1.call-done, f32[8,512]{1,0:T(8,128)S(1)} %psum.15), kind=kLoop, calls=%fused_computation.24 | loop fusion | flops 6029312 | bytes 7618560 | tf_op jit(solution)/shard_map/div | solution.py:107
  (18 shorter events, 0.5 us)
Async XLA Ops:
  6.5 218.9 %all-reduce.7.cloned.1.call-start = ((), (), s32[]{:S(2)}) async-start(), calls=%async_computation.1 | async-start | bytes 1572864
  11.0 2.5 copy-start
  17.9 3.4 copy-start.2
  21.2 4.5 %copy-start.1 = (f32[1,1,1,64,48]{3,4,2,1,0:T(8,128)S(1)}, f32[1,1,1,64,48]{3,4,2,1,0:T(8,128)}, u32[]{:S(2)}) copy-start(f32[1,1,1,64,48]{3,4,2,1,0:T(8,128)} %param.7) | copy-start | bytes 36868
  25.6 360.6 %all-reduce.5.cloned.1.call-start = ((), (), s32[]{:S(2)}) async-start(), calls=%async_computation | async-start | bytes 2097152 | tf_op jit(solution)/shard_map/psum | solution.py:106
  305.9 37.9 %collective-permute-start = (f32[64,1,512]{2,1,0:T(1,128)}, f32[64,1,512]{2,1,0:T(1,128)S(1)}, u32[]{:S(2)}, u32[]{:S(2)}) collective-permute-start(f32[64,1,512]{2,1,0:T(1,128)} %get-tuple-element.7), channel_id=1, source_target_pairs={{0,8},{8,16},{16,24},{24,32},{32,40},{40,48},{48,56},{56,64},{64,7... | collective-permute-start | bytes 393224 | tf_op jit(solution)/shard_map/ppermute | solution.py:17
  308.2 35.7 %collective-permute-start.1 = (f32[64,1,512]{2,1,0:T(1,128)}, f32[64,1,512]{2,1,0:T(1,128)S(1)}, u32[]{:S(2)}, u32[]{:S(2)}) collective-permute-start(f32[64,1,512]{2,1,0:T(1,128)} %get-tuple-element.8), channel_id=1, source_target_pairs={{8,0},{16,8},{24,16},{32,24},{40,32},{48,40},{56,48},{64,56},{72,6... | collective-permute-start | bytes 393224 | tf_op jit(solution)/shard_map/ppermute | solution.py:18
Sparse Core Ops, SparseCore 0:
  25.7 199.6 all-reduce.6
  303.6 82.5 all-reduce.4
where the time goes:
time: 398 us
  waiting for transfers between devices  238 us (60%)
  blocking collectives  79.7 us (20%)
  local copies, waits for them, and re-layouts  27.2 us (7%)
  matrix products  23.7 us (6%)
  between operations  13.5 us (3%)
  other arithmetic  9.96 us (3%)
  starting transfers between devices  5.81 us (1%)
    unnamed x3, waiting for transfers between devices  198 us
    all_gather x1, blocking collectives, per_device(): every_block = lax.all_gather(ratios, 'tile', axis=0, tiled=True)  48.9 us
    psum x1, waiting for transfers between devices, per_device(): back_total, sens_total = lax.psum((back_sum, sensitivity), 'view')  39.3 us
    psum x1, blocking collectives, per_device(): back_total, sens_total = lax.psum((back_sum, sensitivity), 'view')  30.8 us
    dot_general x1, matrix products, per_device(): jnp.einsum('sq,spx->pqx', segment_onehot, spread_back, precision=high)  8.51 us
  transfers between devices with their start and end apart: 4, of which 2 were waited for; matrix products, arithmetic and copies ran while one was open for 2% of the time, Pallas kernels for 0%

commit v1 on v0

v1 whole, which is shorter than its diff:
```python
import functools

import jax
import jax.numpy as jnp
from jax import lax
from jax.experimental import pallas as pl
from jax.experimental.pallas import tpu as pltpu
from jax.sharding import PartitionSpec as P

BACKGROUND = 1.0
HUBER_DELTA = 0.1
LANES = 128
UNROLL = 8
MESH = pl.DeviceIdType.MESH
VMEM_LIMIT = 24 * 1024 * 1024


def lane_block(shape, width):
    return lax.broadcasted_iota(jnp.int32, shape, len(shape) - 1) // width


def swap_chunks(parts, width):
    chunks = len(parts)
    which = lane_block(parts[0].shape, width)
    outs = []
    for i in range(chunks):
        out = parts[i]
        for j in range(chunks):
            if j != i:
                moved = pltpu.roll(parts[j], ((j - i) * width) % LANES, 1)
                out = jnp.where(which == j, moved, out)
        outs.append(out)
    return outs


def forward_kernel(dims, cross_ref, counts_ref, vol_ref, w_ref, dense_ref, edges_ref, vol, segs, acc):
    planes, rows, cols, seg_cols, views, slots, blocks_view, bins, pc = dims
    per_group = LANES // seg_cols
    half = bins // 2
    total_blocks = views * blocks_view
    first_plane = lax.axis_index("view") * pc
    base = pl.multiple_of(first_plane * rows, rows)
    for g in range(cols // LANES):
        group = slice(LANES * g, LANES * (g + 1))
        vol[g] = vol_ref[:, group]
        edges_ref[0, :, group] = vol[g, pl.ds(base + rows - 1, pc, stride=rows), :]
        edges_ref[1, :, group] = vol[g, pl.ds(base, pc, stride=rows), :]
        for h in range(rows // per_group):
            parts = [
                vol[g, pl.ds(per_group * h + i, planes, stride=rows), :]
                for i in range(per_group)
            ]
            for j, out in enumerate(swap_chunks(parts, seg_cols)):
                out = out.astype(jnp.bfloat16)
                lanes = slice(LANES * h, LANES * (h + 1))
                segs[per_group * g + j, 0:planes, lanes] = out
                segs[per_group * g + j, planes : 2 * planes, lanes] = out
    acc[...] = jnp.zeros_like(acc)
    low = lax.broadcasted_iota(jnp.int32, (half, LANES), 1) < planes

    for w in range(views):
        count = counts_ref[w]

        def body(step, carry, w=w, count=count):
            packed = []
            for u in range(UNROLL):
                k = step * UNROLL + u
                seg = cross_ref[w * 2 * slots + slots + k]
                part = lax.dot_general(
                    w_ref[w * slots + k],
                    segs[seg],
                    (((1,), (1,)), ((), ())),
                    preferred_element_type=jnp.float32,
                )
                packed.append(jnp.where(low, part[:half], part[half:]))
            for u in range(UNROLL):
                k = step * UNROLL + u
                block = cross_ref[w * 2 * slots + k] + w * blocks_view
                at = jnp.where(k < count, block, total_blocks)
                acc[at] += packed[u]
            return carry

        lax.fori_loop(0, (count + UNROLL - 1) // UNROLL, body, 0)
    dense_ref[...] = acc[0:total_blocks].astype(jnp.bfloat16)


def exchange_kernel(
    n_tile, dense_ref, meas_ref, edges_ref, ratios_ref, halo_ref, recv,
    send_sem, recv_sem, gsend_sem, grecv_sem, hsend_sem, hrecv_sem,
):
    me = lax.axis_index("tile")
    view = lax.axis_index("view")
    planes = meas_ref.shape[1]
    half = meas_ref.shape[0] // 2

    def peer_of(k):
        return lax.rem(me + k, n_tile)

    barrier = pltpu.get_barrier_semaphore()

    def greet(k, carry):
        pl.semaphore_signal(barrier, inc=1, device_id=(peer_of(k), view), device_id_type=MESH)
        return carry

    lax.fori_loop(1, n_tile, greet, 0)
    pl.semaphore_wait(barrier, n_tile - 1)

    def send(k, carry):
        peer = peer_of(k)
        pltpu.make_async_remote_copy(
            src_ref=dense_ref.at[peer],
            dst_ref=recv.at[k],
            send_sem=send_sem,
            recv_sem=recv_sem,
            device_id=(peer, view),
            device_id_type=MESH,
        ).start()
        return carry

    lax.fori_loop(1, n_tile, send, 0)
    halos = []
    for side, step in ((0, 1), (1, n_tile - 1)):
        halos.append(
            pltpu.make_async_remote_copy(
                src_ref=edges_ref.at[side],
                dst_ref=halo_ref.at[side],
                send_sem=hsend_sem.at[side],
                recv_sem=hrecv_sem.at[side],
                device_id=(peer_of(step), view),
                device_id_type=MESH,
            )
        )
        halos[-1].start()
    low = lax.broadcasted_iota(jnp.int32, (half, LANES), 1) < planes
    counted = jnp.concatenate([meas_ref[...], meas_ref[...]], axis=1)
    counted = jnp.where(low, counted[:half], counted[half:])
    own = dense_ref[me].astype(jnp.float32)
    rest = pl.ds(1, n_tile - 1)
    pltpu.make_async_copy(recv.at[rest], recv.at[rest], recv_sem).wait()
    total = own
    for k in range(1, n_tile):
        total = total + recv[k].astype(jnp.float32)
    ratio = (counted / (total + BACKGROUND)).astype(jnp.bfloat16)
    ratios_ref[me] = ratio

    def spread(k, carry):
        pltpu.make_async_remote_copy(
            src_ref=ratios_ref.at[me],
            dst_ref=ratios_ref.at[me],
            send_sem=gsend_sem,
            recv_sem=grecv_sem,
            device_id=(peer_of(k), view),
            device_id_type=MESH,
        ).start()
        return carry

    lax.fori_loop(1, n_tile, spread, 0)
    pltpu.make_async_copy(recv.at[rest], recv.at[rest], grecv_sem).wait()
    pltpu.make_async_copy(recv.at[rest], recv.at[rest], send_sem).wait()
    pltpu.make_async_copy(recv.at[rest], recv.at[rest], gsend_sem).wait()
    for copy in halos:
        copy.wait()


def backward_kernel(dims, cross_ref, counts_ref, ratios_ref, w_ref, back_ref, sens_ref, lhs, acc):
    planes, rows, cols, seg_cols, views, slots, blocks_view, bins, pc = dims
    total_blocks = views * blocks_view
    chunks = planes // pc

    def fill(step, carry):
        for u in range(UNROLL):
            b = step * UNROLL + u
            x = ratios_ref[b].astype(jnp.float32)
            x = jnp.concatenate([x, pltpu.roll(x, planes, 1)], axis=0)
            lhs[b, 0:planes] = jnp.transpose(x)[0:planes].astype(jnp.bfloat16)
            lhs[b, planes:] = jnp.ones((lhs.shape[1] - planes, bins), jnp.bfloat16)
        return carry

    lax.fori_loop(0, total_blocks // UNROLL, fill, 0)
    lhs[total_blocks] = jnp.zeros(lhs.shape[1:], jnp.bfloat16)
    acc[...] = jnp.zeros_like(acc)
    for w in range(views):
        count = counts_ref[w]

        def body(step, carry, w=w, count=count):
            spread = []
            for u in range(UNROLL):
                k = step * UNROLL + u
                block = cross_ref[w * 2 * slots + k] + w * blocks_view
                at = jnp.where(k < count, block, total_blocks)
                spread.append(
                    jnp.dot(lhs[at], w_ref[w * slots + k], preferred_element_type=jnp.float32)
                )
            for u in range(UNROLL):
                seg = cross_ref[w * 2 * slots + slots + step * UNROLL + u]
                acc[seg] += spread[u]
            return carry

        lax.fori_loop(0, (count + UNROLL - 1) // UNROLL, body, 0)
    for q in range(acc.shape[0]):
        for c in range(chunks):
            back_ref[c, q] = acc[q, c * pc : (c + 1) * pc].astype(jnp.bfloat16)
        sens_ref[q : q + 1] = acc[q, planes : planes + 1]


def update_kernel(
    sizes, back_ref, sens_ref, vol_ref, halo_ref, out_ref, rback, rsens, natural,
    send_sem, recv_sem, ssend_sem, srecv_sem, gsend_sem, grecv_sem,
):
    n_tile, n_view, seg_cols = sizes
    tile = lax.axis_index("tile")
    me = lax.axis_index("view")
    planes, rows, cols = vol_ref.shape
    pc = planes // n_view
    per_group = LANES // seg_cols

    def peer_of(k):
        return lax.rem(me + k, n_view)

    barrier = pltpu.get_barrier_semaphore()
    for k in range(1, n_view):
        pl.semaphore_signal(barrier, inc=1, device_id=(tile, peer_of(k)), device_id_type=MESH)
    pl.semaphore_wait(barrier, n_view - 1)
    copies = []
    for k in range(1, n_view):
        for src, dst, ss, rs in (
            (sens_ref, rsens.at[k], ssend_sem.at[k], srecv_sem.at[k]),
            (back_ref.at[peer_of(k)], rback.at[k], send_sem.at[k], recv_sem.at[k]),
        ):
            copies.append(
                pltpu.make_async_remote_copy(
                    src_ref=src, dst_ref=dst, send_sem=ss, recv_sem=rs,
                    device_id=(tile, peer_of(k)), device_id_type=MESH,
                )
            )
            copies[-1].start()
    first = pl.multiple_of(me * pc, pc)
    v = vol_ref[pl.ds(first, pc)]
    before = vol_ref[jnp.maximum(first - 1, 0)]
    before = jnp.where(me > 0, before, 0.0)
    after = vol_ref[jnp.minimum(first + pc, planes - 1)]
    after = jnp.where(me < n_view - 1, after, 0.0)
    row = lax.broadcasted_iota(jnp.int32, (pc, rows, cols), 1)
    col = lax.broadcasted_iota(jnp.int32, (pc, rows, cols), 2)
    above = jnp.where(tile > 0, halo_ref[0], 0.0)[:, None, :]
    below = jnp.where(tile < n_tile - 1, halo_ref[1], 0.0)[:, None, :]

    def term(other):
        return jnp.clip(v - other, -HUBER_DELTA, HUBER_DELTA)

    penalty = term(jnp.concatenate([before[None], v[: pc - 1]], axis=0))
    penalty += term(jnp.concatenate([v[1:], after[None]], axis=0))
    penalty += term(jnp.where(row == 0, above, pltpu.roll(v, 1, 1)))
    penalty += term(jnp.where(row == rows - 1, below, pltpu.roll(v, rows - 1, 1)))
    penalty += term(jnp.where(col == 0, 0.0, pltpu.roll(v, 1, 2)))
    penalty += term(jnp.where(col == cols - 1, 0.0, pltpu.roll(v, cols - 1, 2)))
    scale = v / (1.0 + penalty)

    for copy in copies:
        copy.wait_recv()
    sens = sens_ref[...]
    for k in range(1, n_view):
        sens = sens + rsens[k]
    for g in range(cols // LANES):
        parts = []
        for j in range(per_group):
            q = per_group * g + j
            total = back_ref[me, q].astype(jnp.float32)
            for k in range(1, n_view):
                total = total + rback[k, q].astype(jnp.float32)
            parts.append(total / sens[q : q + 1])
        for h in range(rows // per_group):
            lanes = slice(LANES * h, LANES * (h + 1))
            for i, out in enumerate(swap_chunks([x[:, lanes] for x in parts], seg_cols)):
                natural[g, pl.ds(per_group * h + i, pc, stride=rows), :] = out
    for g in range(cols // LANES):
        lanes = slice(LANES * g, LANES * (g + 1))
        out_ref[pl.ds(first, pc), :, lanes] = scale[:, :, lanes] * natural[g].reshape(
            pc, rows, LANES
        )
    mine = out_ref.at[pl.ds(first, pc)]
    final = []
    for k in range(1, n_view):
        final.append(
            pltpu.make_async_remote_copy(
                src_ref=mine, dst_ref=mine, send_sem=gsend_sem.at[k], recv_sem=grecv_sem.at[k],
                device_id=(tile, peer_of(k)), device_id_type=MESH,
            )
        )
        final[-1].start()
    for copy in copies:
        copy.wait_send()
    for copy in final:
        copy.wait()


def per_device(volume, weights, measured, crossings, counts):
    n_tile = lax.axis_size("tile")
    n_view = lax.axis_size("view")
    planes, rows, cols = volume.shape
    views, slots, bins, seg_pixels = weights.shape[1:]
    seg_cols = seg_pixels // rows
    seg_total = cols // seg_cols
    blocks_view = n_tile // views
    pc = planes // n_view
    half = bins // 2
    total = views * blocks_view
    dims = (planes, rows, cols, seg_cols, views, slots, blocks_view, bins, pc)
    f32, bf16 = jnp.float32, jnp.bfloat16
    vmem = pl.BlockSpec(memory_space=pltpu.VMEM)
    smem = pl.BlockSpec(memory_space=pltpu.SMEM)
    dma = pltpu.SemaphoreType.DMA
    local = pltpu.CompilerParams(vmem_limit_bytes=VMEM_LIMIT)

    def remote(number):
        return pltpu.CompilerParams(
            vmem_limit_bytes=VMEM_LIMIT, collective_id=number, has_side_effects=True
        )

    cross = crossings[0].transpose(0, 2, 1).reshape(views * 2 * slots)
    count = counts[0]
    slot_weights = weights.reshape(views * slots, bins, seg_pixels)
    dense, edges = pl.pallas_call(
        functools.partial(forward_kernel, dims),
        out_shape=(
            jax.ShapeDtypeStruct((total, half, LANES), bf16),
            jax.ShapeDtypeStruct((2, pc, cols), f32),
        ),
        in_specs=[smem, smem, vmem, vmem],
        out_specs=(vmem, vmem),
        scratch_shapes=[
            pltpu.VMEM((cols // LANES, planes * rows, LANES), f32),
            pltpu.VMEM((seg_total, 2 * planes, seg_pixels), bf16),
            pltpu.VMEM((total + 1, half, LANES), f32),
        ],
        compiler_params=local,
        name="forward",
    )(cross, count, volume.reshape(planes * rows, cols), slot_weights)
    ratios, halo = pl.pallas_call(
        functools.partial(exchange_kernel, n_tile),
        out_shape=(
            jax.ShapeDtypeStruct((total, half, LANES), bf16),
            jax.ShapeDtypeStruct((2, pc, cols), f32),
        ),
        in_specs=[vmem, vmem, vmem],
        out_specs=(vmem, vmem),
        scratch_shapes=[
            pltpu.VMEM((n_tile, half, LANES), bf16),
            dma, dma, dma, dma, dma((2,)), dma((2,)),
        ],
        compiler_params=remote(1),
        name="exchange",
    )(dense, measured[0, 0, 0].T, edges)
    back, sens = pl.pallas_call(
        functools.partial(backward_kernel, dims),
        out_shape=(
            jax.ShapeDtypeStruct((n_view, seg_total, pc, seg_pixels), bf16),
            jax.ShapeDtypeStruct((seg_total, seg_pixels), f32),
        ),
        in_specs=[smem, smem, vmem, vmem],
        out_specs=(vmem, vmem),
        scratch_shapes=[
            pltpu.VMEM((total + 1, planes + 8, bins), bf16),
            pltpu.VMEM((seg_total, planes + 8, seg_pixels), f32),
        ],
        compiler_params=local,
        name="backward",
    )(cross, count, ratios, slot_weights)
    return pl.pallas_call(
        functools.partial(update_kernel, (n_tile, n_view, seg_cols)),
        out_shape=jax.ShapeDtypeStruct((planes, rows, cols), f32),
        in_specs=[vmem, vmem, vmem, vmem],
        out_specs=vmem,
        scratch_shapes=[
            pltpu.VMEM((n_view, seg_total, pc, seg_pixels), bf16),
            pltpu.VMEM((n_view, seg_total, seg_pixels), f32),
            pltpu.VMEM((cols // LANES, pc * rows, LANES), f32),
        ]
        + [dma((n_view,))] * 6,
        compiler_params=remote(2),
        name="update",
    )(back, sens, volume, halo)


def solution(mesh):
    in_specs = (
        P(None, "tile", None),
        P("tile", "view", None, None, None),
        P("tile", "view", None, None, None),
        P("tile", "view", None, None),
        P("tile", "view"),
    )
    out_specs = P(None, "tile", None)
    return jax.shard_map(
        per_device, mesh=mesh, in_specs=in_specs, out_specs=out_specs, check_vma=False
    )
```

time: 398 us -> 104 us (0.26)
  the two profiles are of different devices: /device:TPU:6 before, /device:TPU:146 now
where the time goes in v1:
time: 104 us
  Pallas kernels  97.5 us (94%)
  local copies, waits for them, and re-layouts  6.25 us (6%)
    pallas_call x1, Pallas kernels, per_device(): pl.pallas_call(functools.partial(update_kernel, (n_tile, n_view, seg_cols...  53.7 us
    pallas_call x1, Pallas kernels, per_device(): pl.pallas_call(functools.partial(exchange_kernel, n_tile), out_shape=(jax...  31.7 us
    pallas_call x1, Pallas kernels, per_device(): pl.pallas_call(functools.partial(backward_kernel, dims), out_shape=(jax.S...  6.28 us
    pallas_call x1, Pallas kernels, per_device(): pl.pallas_call(functools.partial(forward_kernel, dims), out_shape=(jax.Sh...  5.78 us
    unnamed x13, local copies, waits for them, and re-layouts  5.48 us

profile of v1, /device:TPU:146, one launch (start us, length us, event | category | flops | bytes accessed | tf_op | source)
XLA Modules:
  0.0 103.8 jit_solution(9479658658393580539)
XLA Ops:
  0.0 0.8 reshape.9.cross_ref
  0.8 0.0 copy-start
  0.8 1.9 %copy-done = bf16[1,4,32,48,256]{4,3,2,1,0:T(8,128)(2,1)S(1)} copy-done((bf16[1,4,32,48,256]{4,3,2,1,0:T(8,128)(2,1)S(1)}, bf16[1,4,32,48,256]{4,3,2,1,0:T(8,128)(2,1)}, u32[]{:S(2)}) %copy-start) | copy-done | bytes 3145752
  2.7 0.0 copy-start.2
  2.7 1.2 %copy-done.2 = f32[64,8,512]{2,1,0:T(8,128)S(1)} copy-done((f32[64,8,512]{2,1,0:T(8,128)S(1)}, f32[64,8,512]{2,1,0:T(8,128)}, u32[]{:S(2)}) %copy-start.2) | copy-done | bytes 1048600
  3.9 0.0 copy-start.5
  3.9 0.7 copy-done.5
  4.5 0.0 copy-start.1
  4.5 0.0 copy-start.3
  4.5 5.8 %forward.1 = (bf16[64,24,128]{2,1,0:T(8,128)(2,1)S(1)}, f32[2,8,512]{2,1,0:T(8,128)S(1)}) custom-call(s32[256]{0:T(256)S(1)} %reshape.9.cross_ref, s32[4]{0:T(128)S(1)} %bitcast.13, f32[512,512]{1,0:T(8,128)S(1)} %bitcast.11, bf16[128,48,256]{2,1,0:T(8,128)(2,1)S(1)} %bitcast.9), custom_call_target="tpu_custom_call" | custom-call | tf_op jit(solution)/shard_map/forward/pallas_call | solution.py:323
  10.3 0.0 copy-start.4
  10.3 0.7 copy-done.4
  11.1 31.7 %exchange.1 = (bf16[64,24,128]{2,1,0:T(8,128)(2,1)S(1)}, f32[2,8,512]{2,1,0:T(8,128)S(1)}) custom-call(bf16[64,24,128]{2,1,0:T(8,128)(2,1)S(1)} %get-tuple-element.11.dense_ref, f32[48,64]{1,0:T(8,128)S(1)} %bitcast.12, f32[2,8,512]{2,1,0:T(8,128)S(1)} %get-tuple-element.12.edges_ref), custom_call_target="tpu_custom_call" | custom-call | tf_op jit(solution)/shard_map/exchange/pallas_call | solution.py:339
  42.8 0.0 copy-done.1
  42.8 6.3 %backward.1 = (bf16[8,16,8,256]{3,2,1,0:T(8,128)(2,1)S(1)}, f32[16,256]{1,0:T(8,128)S(1)}) custom-call(s32[256]{0:T(256)S(1)} %reshape.9.cross_ref, s32[4]{0:T(128)S(1)} %bitcast.14, bf16[64,24,128]{2,1,0:T(8,128)(2,1)S(1)} %get-tuple-element.13.ratios_ref, bf16[128,48,256]{2,1,0:T(8,128)(2,1)S(1)} %bitcast.10), custom_call_target="tpu_custom_call" | custom-call | tf_op jit(solution)/shard_map/backward/pallas_call | solution.py:354
  49.1 0.0 copy-done.3
  49.1 53.7 %update.1 = f32[64,8,512]{2,1,0:T(8,128)S(1)} custom-call(bf16[8,16,8,256]{3,2,1,0:T(8,128)(2,1)S(1)} %get-tuple-element.14.back_ref, f32[16,256]{1,0:T(8,128)S(1)} %get-tuple-element.15.sens_ref, f32[64,8,512]{2,1,0:T(8,128)S(1)} %copy-done.3, f32[2,8,512]{2,1,0:T(8,128)S(1)} %get-tuple-element.16.halo_ref), custom_call_target="tpu_custom_call" | custom-call | tf_op jit(solution)/shard_map/update/pallas_call | solution.py:369
  102.8 1.0 copy.7
Async XLA Ops:
  0.8 1.9 %copy-start = (bf16[1,4,32,48,256]{4,3,2,1,0:T(8,128)(2,1)S(1)}, bf16[1,4,32,48,256]{4,3,2,1,0:T(8,128)(2,1)}, u32[]{:S(2)}) copy-start(bf16[1,4,32,48,256]{4,3,2,1,0:T(8,128)(2,1)} %param.6) | copy-start | bytes 9437188
  2.7 1.2 %copy-start.2 = (f32[64,8,512]{2,1,0:T(8,128)S(1)}, f32[64,8,512]{2,1,0:T(8,128)}, u32[]{:S(2)}) copy-start(f32[64,8,512]{2,1,0:T(8,128)} %vol_ref.1) | copy-start | bytes 3145732
  3.9 0.7 copy-start.5
  4.5 38.3 %copy-start.1 = (bf16[1,4,32,48,256]{4,3,2,1,0:T(8,128)(2,1)S(1)}, bf16[1,4,32,48,256]{4,3,2,1,0:T(8,128)(2,1)}, u32[]{:S(2)}) copy-start(bf16[1,4,32,48,256]{4,3,2,1,0:T(8,128)(2,1)} %param.6) | copy-start | bytes 9437188
  4.5 44.6 %copy-start.3 = (f32[64,8,512]{2,1,0:T(8,128)S(1)}, f32[64,8,512]{2,1,0:T(8,128)}, u32[]{:S(2)}) copy-start(f32[64,8,512]{2,1,0:T(8,128)} %vol_ref.1) | copy-start | bytes 3145732
  10.3 0.7 copy-start.4

commit v2 on v1

--- a/solution.py
+++ b/solution.py
@@ -217,23 +217,30 @@
     def peer_of(k):
         return lax.rem(me + k, n_view)
 
+    def push(src, dst, send, recv, k):
+        copy = pltpu.make_async_remote_copy(
+            src_ref=src, dst_ref=dst, send_sem=send, recv_sem=recv,
+            device_id=(tile, peer_of(k)), device_id_type=MESH,
+        )
+        copy.start()
+        return copy
+
     barrier = pltpu.get_barrier_semaphore()
     for k in range(1, n_view):
         pl.semaphore_signal(barrier, inc=1, device_id=(tile, peer_of(k)), device_id_type=MESH)
     pl.semaphore_wait(barrier, n_view - 1)
-    copies = []
-    for k in range(1, n_view):
-        for src, dst, ss, rs in (
-            (sens_ref, rsens.at[k], ssend_sem.at[k], srecv_sem.at[k]),
-            (back_ref.at[peer_of(k)], rback.at[k], send_sem.at[k], recv_sem.at[k]),
-        ):
-            copies.append(
-                pltpu.make_async_remote_copy(
-                    src_ref=src, dst_ref=dst, send_sem=ss, recv_sem=rs,
-                    device_id=(tile, peer_of(k)), device_id_type=MESH,
-                )
+    groups = cols // LANES
+    order = sorted(range(1, n_view), key=lambda k: -min(k, n_view - k))
+    sens_copies, copies = [], {}
+    for k in order:
+        sens_copies.append(push(sens_ref, rsens.at[k], ssend_sem.at[k], srecv_sem.at[k], k))
+    for g in range(groups):
+        piece = pl.ds(per_group * g, per_group)
+        for k in order:
+            copies[g, k] = push(
+                back_ref.at[peer_of(k), piece], rback.at[k, piece],
+                send_sem.at[g, k], recv_sem.at[g, k], k,
             )
-            copies[-1].start()
     first = pl.multiple_of(me * pc, pc)
     v = vol_ref[pl.ds(first, pc)]
     before = vol_ref[jnp.maximum(first - 1, 0)]
@@ -256,12 +263,15 @@
     penalty += term(jnp.where(col == cols - 1, 0.0, pltpu.roll(v, cols - 1, 2)))
     scale = v / (1.0 + penalty)
 
-    for copy in copies:
+    for copy in sens_copies:
         copy.wait_recv()
     sens = sens_ref[...]
     for k in range(1, n_view):
         sens = sens + rsens[k]
-    for g in range(cols // LANES):
+
+    def finish(g):
+        for k in order:
+            copies[g, k].wait_recv()
         parts = []
         for j in range(per_group):
             q = per_group * g + j
@@ -273,25 +283,45 @@
             lanes = slice(LANES * h, LANES * (h + 1))
             for i, out in enumerate(swap_chunks([x[:, lanes] for x in parts], seg_cols)):
                 natural[g, pl.ds(per_group * h + i, pc, stride=rows), :] = out
-    for g in range(cols // LANES):
         lanes = slice(LANES * g, LANES * (g + 1))
         out_ref[pl.ds(first, pc), :, lanes] = scale[:, :, lanes] * natural[g].reshape(
             pc, rows, LANES
         )
-    mine = out_ref.at[pl.ds(first, pc)]
-    final = []
-    for k in range(1, n_view):
-        final.append(
-            pltpu.make_async_remote_copy(
-                src_ref=mine, dst_ref=mine, send_sem=gsend_sem.at[k], recv_sem=grecv_sem.at[k],
-                device_id=(tile, peer_of(k)), device_id_type=MESH,
-            )
+
+    def piece_of(owner, g):
+        return out_ref.at[pl.ds(pl.multiple_of(owner * pc, pc), pc), :, LANES * g : LANES * (g + 1)]
+
+    far = n_view // 2
+    relays = {}
+
+    def relay(side, hop, g):
+        owner = lax.rem(me + (n_view - hop if side == 0 else hop), n_view)
+        piece = piece_of(owner, g)
+        relays[side, hop, g] = push(
+            piece, piece, gsend_sem.at[side, hop, g], grecv_sem.at[side, hop, g],
+            1 if side == 0 else n_view - 1,
         )
-        final[-1].start()
-    for copy in copies:
+
+    def reach(side, g):
+        return far if (side == 0) == (g < groups // 2) else n_view - 1 - far
+
+    for tick in range(groups + far):
+        for g in range(groups):
+            hop = tick - g
+            if hop == 0:
+                finish(g)
+                for side in (0, 1):
+                    relay(side, 0, g)
+            elif 1 <= hop <= far:
+                for side in (0, 1):
+                    if hop <= reach(side, g):
+                        relays[side, hop - 1, g].wait_recv()
+                        if hop < reach(side, g):
+                            relay(side, hop, g)
+    for copy in sens_copies:
         copy.wait_send()
-    for copy in final:
-        copy.wait()
+    for copy in list(copies.values()) + list(relays.values()):
+        copy.wait_send()
 
 
 def per_device(volume, weights, measured, crossings, counts):
@@ -376,7 +406,9 @@
             pltpu.VMEM((n_view, seg_total, seg_pixels), f32),
             pltpu.VMEM((cols // LANES, pc * rows, LANES), f32),
         ]
-        + [dma((n_view,))] * 6,
+        + [dma((cols // LANES, n_view))] * 2
+        + [dma((n_view,))] * 2
+        + [dma((2, n_view // 2, cols // LANES))] * 2,
         compiler_params=remote(2),
         name="update",
     )(back, sens, volume, halo)

time: 104 us -> 102 us (0.981)
  the two profiles are of different devices: /device:TPU:146 before, /device:TPU:6 now
where the time goes in v2:
time: 102 us; the launch traced here: 101 us
  Pallas kernels  94.2 us (92%)
  local copies, waits for them, and re-layouts  6.25 us (6%)
    pallas_call x1, Pallas kernels, per_device(): pl.pallas_call(functools.partial(update_kernel, (n_tile, n_view, seg_cols...  47.4 us
    pallas_call x1, Pallas kernels, per_device(): pl.pallas_call(functools.partial(exchange_kernel, n_tile), out_shape=(jax...  34.3 us
    pallas_call x1, Pallas kernels, per_device(): pl.pallas_call(functools.partial(backward_kernel, dims), out_shape=(jax.S...  6.51 us
    pallas_call x1, Pallas kernels, per_device(): pl.pallas_call(functools.partial(forward_kernel, dims), out_shape=(jax.Sh...  6.05 us
    unnamed x13, local copies, waits for them, and re-layouts  5.48 us

profile of v2, /device:TPU:6, one launch (start us, length us, event | category | flops | bytes accessed | tf_op | source)
XLA Modules:
  0.0 100.5 jit_solution(11778758745791556819)
XLA Ops:
  0.0 0.8 reshape.9.cross_ref
  0.8 0.0 copy-start
  0.8 1.9 %copy-done = bf16[1,4,32,48,256]{4,3,2,1,0:T(8,128)(2,1)S(1)} copy-done((bf16[1,4,32,48,256]{4,3,2,1,0:T(8,128)(2,1)S(1)}, bf16[1,4,32,48,256]{4,3,2,1,0:T(8,128)(2,1)}, u32[]{:S(2)}) %copy-start) | copy-done | bytes 3145752
  2.7 0.0 copy-start.2
  2.7 1.2 %copy-done.2 = f32[64,8,512]{2,1,0:T(8,128)S(1)} copy-done((f32[64,8,512]{2,1,0:T(8,128)S(1)}, f32[64,8,512]{2,1,0:T(8,128)}, u32[]{:S(2)}) %copy-start.2) | copy-done | bytes 1048600
  3.9 0.0 copy-start.5
  3.9 0.7 copy-done.5
  4.5 0.0 copy-start.1
  4.5 0.0 copy-start.3
  4.5 6.0 %forward.1 = (bf16[64,24,128]{2,1,0:T(8,128)(2,1)S(1)}, f32[2,8,512]{2,1,0:T(8,128)S(1)}) custom-call(s32[256]{0:T(256)S(1)} %reshape.9.cross_ref, s32[4]{0:T(128)S(1)} %bitcast.13, f32[512,512]{1,0:T(8,128)S(1)} %bitcast.11, bf16[128,48,256]{2,1,0:T(8,128)(2,1)S(1)} %bitcast.9), custom_call_target="tpu_custom_call" | custom-call | tf_op jit(solution)/shard_map/forward/pallas_call | solution.py:353
  10.6 0.0 copy-start.4
  10.6 0.7 copy-done.4
  11.3 34.3 %exchange.1 = (bf16[64,24,128]{2,1,0:T(8,128)(2,1)S(1)}, f32[2,8,512]{2,1,0:T(8,128)S(1)}) custom-call(bf16[64,24,128]{2,1,0:T(8,128)(2,1)S(1)} %get-tuple-element.11.dense_ref, f32[48,64]{1,0:T(8,128)S(1)} %bitcast.12, f32[2,8,512]{2,1,0:T(8,128)S(1)} %get-tuple-element.12.edges_ref), custom_call_target="tpu_custom_call" | custom-call | tf_op jit(solution)/shard_map/exchange/pallas_call | solution.py:369
  45.7 0.0 copy-done.1
  45.7 6.5 %backward.1 = (bf16[8,16,8,256]{3,2,1,0:T(8,128)(2,1)S(1)}, f32[16,256]{1,0:T(8,128)S(1)}) custom-call(s32[256]{0:T(256)S(1)} %reshape.9.cross_ref, s32[4]{0:T(128)S(1)} %bitcast.14, bf16[64,24,128]{2,1,0:T(8,128)(2,1)S(1)} %get-tuple-element.13.ratios_ref, bf16[128,48,256]{2,1,0:T(8,128)(2,1)S(1)} %bitcast.10), custom_call_target="tpu_custom_call" | custom-call | tf_op jit(solution)/shard_map/backward/pallas_call | solution.py:384
  52.2 0.0 copy-done.3
  52.2 47.4 %update.1 = f32[64,8,512]{2,1,0:T(8,128)S(1)} custom-call(bf16[8,16,8,256]{3,2,1,0:T(8,128)(2,1)S(1)} %get-tuple-element.14.back_ref, f32[16,256]{1,0:T(8,128)S(1)} %get-tuple-element.15.sens_ref, f32[64,8,512]{2,1,0:T(8,128)S(1)} %copy-done.3, f32[2,8,512]{2,1,0:T(8,128)S(1)} %get-tuple-element.16.halo_ref), custom_call_target="tpu_custom_call" | custom-call | tf_op jit(solution)/shard_map/update/pallas_call | solution.py:399
  99.6 1.0 copy.7
Async XLA Ops:
  0.8 1.9 %copy-start = (bf16[1,4,32,48,256]{4,3,2,1,0:T(8,128)(2,1)S(1)}, bf16[1,4,32,48,256]{4,3,2,1,0:T(8,128)(2,1)}, u32[]{:S(2)}) copy-start(bf16[1,4,32,48,256]{4,3,2,1,0:T(8,128)(2,1)} %param.6) | copy-start | bytes 9437188
  2.7 1.2 %copy-start.2 = (f32[64,8,512]{2,1,0:T(8,128)S(1)}, f32[64,8,512]{2,1,0:T(8,128)}, u32[]{:S(2)}) copy-start(f32[64,8,512]{2,1,0:T(8,128)} %vol_ref.1) | copy-start | bytes 3145732
  3.9 0.7 copy-start.5
  4.5 41.1 %copy-start.1 = (bf16[1,4,32,48,256]{4,3,2,1,0:T(8,128)(2,1)S(1)}, bf16[1,4,32,48,256]{4,3,2,1,0:T(8,128)(2,1)}, u32[]{:S(2)}) copy-start(bf16[1,4,32,48,256]{4,3,2,1,0:T(8,128)(2,1)} %param.6) | copy-start | bytes 9437188
  4.5 47.6 %copy-start.3 = (f32[64,8,512]{2,1,0:T(8,128)S(1)}, f32[64,8,512]{2,1,0:T(8,128)}, u32[]{:S(2)}) copy-start(f32[64,8,512]{2,1,0:T(8,128)} %vol_ref.1) | copy-start | bytes 3145732
  10.6 0.7 copy-start.4

commit v3 on v2

--- a/solution.py
+++ b/solution.py
@@ -205,7 +205,7 @@
 
 def update_kernel(
     sizes, back_ref, sens_ref, vol_ref, halo_ref, out_ref, rback, rsens, natural,
-    send_sem, recv_sem, ssend_sem, srecv_sem, gsend_sem, grecv_sem,
+    send_sem, ssend_sem, srecv_sem, gsend_sem, recv_sem, grecv_sem,
 ):
     n_tile, n_view, seg_cols = sizes
     tile = lax.axis_index("tile")
@@ -231,16 +231,13 @@
     pl.semaphore_wait(barrier, n_view - 1)
     groups = cols // LANES
     order = sorted(range(1, n_view), key=lambda k: -min(k, n_view - k))
-    sens_copies, copies = [], {}
+    rest = pl.ds(1, n_view - 1)
     for k in order:
-        sens_copies.append(push(sens_ref, rsens.at[k], ssend_sem.at[k], srecv_sem.at[k], k))
+        push(sens_ref, rsens.at[k], ssend_sem, srecv_sem, k)
     for g in range(groups):
         piece = pl.ds(per_group * g, per_group)
         for k in order:
-            copies[g, k] = push(
-                back_ref.at[peer_of(k), piece], rback.at[k, piece],
-                send_sem.at[g, k], recv_sem.at[g, k], k,
-            )
+            push(back_ref.at[peer_of(k), piece], rback.at[k, piece], send_sem, recv_sem.at[g], k)
     first = pl.multiple_of(me * pc, pc)
     v = vol_ref[pl.ds(first, pc)]
     before = vol_ref[jnp.maximum(first - 1, 0)]
@@ -263,15 +260,14 @@
     penalty += term(jnp.where(col == cols - 1, 0.0, pltpu.roll(v, cols - 1, 2)))
     scale = v / (1.0 + penalty)
 
-    for copy in sens_copies:
-        copy.wait_recv()
+    pltpu.make_async_copy(rsens.at[rest], rsens.at[rest], srecv_sem).wait()
     sens = sens_ref[...]
     for k in range(1, n_view):
         sens = sens + rsens[k]
 
     def finish(g):
-        for k in order:
-            copies[g, k].wait_recv()
+        landed = rback.at[rest, pl.ds(per_group * g, per_group)]
+        pltpu.make_async_copy(landed, landed, recv_sem.at[g]).wait()
         parts = []
         for j in range(per_group):
             q = per_group * g + j
@@ -298,30 +294,31 @@
         owner = lax.rem(me + (n_view - hop if side == 0 else hop), n_view)
         piece = piece_of(owner, g)
         relays[side, hop, g] = push(
-            piece, piece, gsend_sem.at[side, hop, g], grecv_sem.at[side, hop, g],
+            piece, piece, gsend_sem, grecv_sem.at[side, hop, g],
             1 if side == 0 else n_view - 1,
         )
 
     def reach(side, g):
         return far if (side == 0) == (g < groups // 2) else n_view - 1 - far
 
-    for tick in range(groups + far):
+    for g in range(groups):
+        finish(g)
+        for side in (0, 1):
+            if reach(side, g) > 0:
+                relay(side, 0, g)
+    for hop in range(1, far + 1):
         for g in range(groups):
-            hop = tick - g
-            if hop == 0:
-                finish(g)
-                for side in (0, 1):
-                    relay(side, 0, g)
-            elif 1 <= hop <= far:
-                for side in (0, 1):
-                    if hop <= reach(side, g):
-                        relays[side, hop - 1, g].wait_recv()
-                        if hop < reach(side, g):
-                            relay(side, hop, g)
-    for copy in sens_copies:
-        copy.wait_send()
-    for copy in list(copies.values()) + list(relays.values()):
-        copy.wait_send()
+            for side in (0, 1):
+                if hop <= reach(side, g):
+                    relays[side, hop - 1, g].wait_recv()
+                    if hop < reach(side, g):
+                        relay(side, hop, g)
+    for sent, sem in (
+        (rsens.at[rest], ssend_sem),
+        (rback.at[rest], send_sem),
+        (out_ref.at[pl.ds(0, planes - pc)], gsend_sem),
+    ):
+        pltpu.make_async_copy(sent, sent, sem).wait()
 
 
 def per_device(volume, weights, measured, crossings, counts):
@@ -406,9 +403,7 @@
             pltpu.VMEM((n_view, seg_total, seg_pixels), f32),
             pltpu.VMEM((cols // LANES, pc * rows, LANES), f32),
         ]
-        + [dma((cols // LANES, n_view))] * 2
-        + [dma((n_view,))] * 2
-        + [dma((2, n_view // 2, cols // LANES))] * 2,
+        + [dma, dma, dma, dma, dma((cols // LANES,)), dma((2, n_view // 2, cols // LANES))],
         compiler_params=remote(2),
         name="update",
     )(back, sens, volume, halo)

time: 102 us -> 92.6 us (0.908)
  Pallas kernels: 94.2 us -> 84.8 us
    pallas_call x1, Pallas kernels: 47.4 us -> 37.9 us  [per_device(): pl.pallas_call(functools.partial(update_kernel, (n_tile, n_view, seg_cols...]
where the time goes in v3:
time: 92.6 us; the launch traced here: 91.1 us
  Pallas kernels  84.8 us (92%)
  local copies, waits for them, and re-layouts  6.25 us (7%)
    pallas_call x1, Pallas kernels, per_device(): pl.pallas_call(functools.partial(update_kernel, (n_tile, n_view, seg_cols...  37.9 us
    pallas_call x1, Pallas kernels, per_device(): pl.pallas_call(functools.partial(exchange_kernel, n_tile), out_shape=(jax...  34.3 us
    pallas_call x1, Pallas kernels, per_device(): pl.pallas_call(functools.partial(backward_kernel, dims), out_shape=(jax.S...  6.51 us
    pallas_call x1, Pallas kernels, per_device(): pl.pallas_call(functools.partial(forward_kernel, dims), out_shape=(jax.Sh...  6.08 us
    unnamed x13, local copies, waits for them, and re-layouts  5.48 us

profile of v3, /device:TPU:6, one launch (start us, length us, event | category | flops | bytes accessed | tf_op | source)
XLA Modules:
  0.0 91.1 jit_solution(5108143098989569557)
XLA Ops:
  0.0 0.8 reshape.9.cross_ref
  0.8 0.0 copy-start
  0.8 1.9 %copy-done = bf16[1,4,32,48,256]{4,3,2,1,0:T(8,128)(2,1)S(1)} copy-done((bf16[1,4,32,48,256]{4,3,2,1,0:T(8,128)(2,1)S(1)}, bf16[1,4,32,48,256]{4,3,2,1,0:T(8,128)(2,1)}, u32[]{:S(2)}) %copy-start) | copy-done | bytes 3145752
  2.7 0.0 copy-start.2
  2.7 1.2 %copy-done.2 = f32[64,8,512]{2,1,0:T(8,128)S(1)} copy-done((f32[64,8,512]{2,1,0:T(8,128)S(1)}, f32[64,8,512]{2,1,0:T(8,128)}, u32[]{:S(2)}) %copy-start.2) | copy-done | bytes 1048600
  3.9 0.0 copy-start.5
  3.9 0.7 copy-done.5
  4.5 0.0 copy-start.1
  4.5 0.0 copy-start.3
  4.5 6.1 %forward.1 = (bf16[64,24,128]{2,1,0:T(8,128)(2,1)S(1)}, f32[2,8,512]{2,1,0:T(8,128)S(1)}) custom-call(s32[256]{0:T(256)S(1)} %reshape.9.cross_ref, s32[4]{0:T(128)S(1)} %bitcast.13, f32[512,512]{1,0:T(8,128)S(1)} %bitcast.11, bf16[128,48,256]{2,1,0:T(8,128)(2,1)S(1)} %bitcast.9), custom_call_target="tpu_custom_call" | custom-call | tf_op jit(solution)/shard_map/forward/pallas_call | solution.py:350
  10.6 0.0 copy-start.4
  10.6 0.7 copy-done.4
  11.4 34.3 %exchange.1 = (bf16[64,24,128]{2,1,0:T(8,128)(2,1)S(1)}, f32[2,8,512]{2,1,0:T(8,128)S(1)}) custom-call(bf16[64,24,128]{2,1,0:T(8,128)(2,1)S(1)} %get-tuple-element.11.dense_ref, f32[48,64]{1,0:T(8,128)S(1)} %bitcast.12, f32[2,8,512]{2,1,0:T(8,128)S(1)} %get-tuple-element.12.edges_ref), custom_call_target="tpu_custom_call" | custom-call | tf_op jit(solution)/shard_map/exchange/pallas_call | solution.py:366
  45.7 0.0 copy-done.1
  45.7 6.5 %backward.1 = (bf16[8,16,8,256]{3,2,1,0:T(8,128)(2,1)S(1)}, f32[16,256]{1,0:T(8,128)S(1)}) custom-call(s32[256]{0:T(256)S(1)} %reshape.9.cross_ref, s32[4]{0:T(128)S(1)} %bitcast.14, bf16[64,24,128]{2,1,0:T(8,128)(2,1)S(1)} %get-tuple-element.13.ratios_ref, bf16[128,48,256]{2,1,0:T(8,128)(2,1)S(1)} %bitcast.10), custom_call_target="tpu_custom_call" | custom-call | tf_op jit(solution)/shard_map/backward/pallas_call | solution.py:381
  52.2 0.0 copy-done.3
  52.2 37.9 %update.1 = f32[64,8,512]{2,1,0:T(8,128)S(1)} custom-call(bf16[8,16,8,256]{3,2,1,0:T(8,128)(2,1)S(1)} %get-tuple-element.14.back_ref, f32[16,256]{1,0:T(8,128)S(1)} %get-tuple-element.15.sens_ref, f32[64,8,512]{2,1,0:T(8,128)S(1)} %copy-done.3, f32[2,8,512]{2,1,0:T(8,128)S(1)} %get-tuple-element.16.halo_ref), custom_call_target="tpu_custom_call" | custom-call | tf_op jit(solution)/shard_map/update/pallas_call | solution.py:396
  90.1 1.0 %copy.7 = f32[64,8,512]{2,1,0:T(8,128)} copy(f32[64,8,512]{2,1,0:T(8,128)S(1)} %update.1) | data formatting | bytes 2097152
Async XLA Ops:
  0.8 1.9 %copy-start = (bf16[1,4,32,48,256]{4,3,2,1,0:T(8,128)(2,1)S(1)}, bf16[1,4,32,48,256]{4,3,2,1,0:T(8,128)(2,1)}, u32[]{:S(2)}) copy-start(bf16[1,4,32,48,256]{4,3,2,1,0:T(8,128)(2,1)} %param.6) | copy-start | bytes 9437188
  2.7 1.2 %copy-start.2 = (f32[64,8,512]{2,1,0:T(8,128)S(1)}, f32[64,8,512]{2,1,0:T(8,128)}, u32[]{:S(2)}) copy-start(f32[64,8,512]{2,1,0:T(8,128)} %vol_ref.1) | copy-start | bytes 3145732
  3.9 0.7 copy-start.5
  4.5 41.1 %copy-start.1 = (bf16[1,4,32,48,256]{4,3,2,1,0:T(8,128)(2,1)S(1)}, bf16[1,4,32,48,256]{4,3,2,1,0:T(8,128)(2,1)}, u32[]{:S(2)}) copy-start(bf16[1,4,32,48,256]{4,3,2,1,0:T(8,128)(2,1)} %param.6) | copy-start | bytes 9437188
  4.5 47.6 %copy-start.3 = (f32[64,8,512]{2,1,0:T(8,128)S(1)}, f32[64,8,512]{2,1,0:T(8,128)}, u32[]{:S(2)}) copy-start(f32[64,8,512]{2,1,0:T(8,128)} %vol_ref.1) | copy-start | bytes 3145732
  10.6 0.7 copy-start.4

commit v4 on v3

--- a/solution.py
+++ b/solution.py
@@ -33,11 +33,26 @@
     return outs
 
 
-def forward_kernel(dims, cross_ref, counts_ref, vol_ref, w_ref, dense_ref, edges_ref, vol, segs, acc):
+def forward_kernel(
+    dims, cross_ref, counts_ref, vol_ref, w_ref, dense_ref, edges_ref, lists_ref, vol, segs, acc, used
+):
     planes, rows, cols, seg_cols, views, slots, blocks_view, bins, pc = dims
     per_group = LANES // seg_cols
     half = bins // 2
     total_blocks = views * blocks_view
+    seg_total = cols // seg_cols
+    room = 2 * views
+    size = seg_total * room + LANES
+    for q in range(seg_total):
+        used[q] = 0
+
+    def clear(i, carry):
+        for u in range(UNROLL):
+            lists_ref[i * UNROLL + u] = 0
+            lists_ref[size + i * UNROLL + u] = total_blocks
+        return carry
+
+    lax.fori_loop(0, seg_total * room // UNROLL, clear, 0)
     first_plane = lax.axis_index("view") * pc
     base = pl.multiple_of(first_plane * rows, rows)
     for g in range(cols // LANES):
@@ -78,6 +93,12 @@
                 block = cross_ref[w * 2 * slots + k] + w * blocks_view
                 at = jnp.where(k < count, block, total_blocks)
                 acc[at] += packed[u]
+                seg = cross_ref[w * 2 * slots + slots + k]
+                place = used[seg]
+                used[seg] = place + jnp.where(k < count, 1, 0)
+                place = jnp.where(k < count, seg * room + place, seg_total * room)
+                lists_ref[place] = w * slots + k
+                lists_ref[size + place] = block
             return carry
 
         lax.fori_loop(0, (count + UNROLL - 1) // UNROLL, body, 0)
@@ -162,10 +183,36 @@
         copy.wait()
 
 
-def backward_kernel(dims, cross_ref, counts_ref, ratios_ref, w_ref, back_ref, sens_ref, lhs, acc):
-    planes, rows, cols, seg_cols, views, slots, blocks_view, bins, pc = dims
-    total_blocks = views * blocks_view
-    chunks = planes // pc
+def update_kernel(
+    sizes, lists_ref, ratios_ref, w_ref, vol_ref, halo_ref, out_ref,
+    lhs, back_ref, sens_ref, rback, rsens, natural,
+    send_sem, ssend_sem, srecv_sem, gsend_sem, recv_sem, grecv_sem,
+):
+    n_tile, n_view, seg_cols, room = sizes
+    tile = lax.axis_index("tile")
+    me = lax.axis_index("view")
+    planes, rows, cols = vol_ref.shape
+    pc = planes // n_view
+    per_group = LANES // seg_cols
+
+    def peer_of(k):
+        return lax.rem(me + k, n_view)
+
+    def push(src, dst, send, recv, k):
+        copy = pltpu.make_async_remote_copy(
+            src_ref=src, dst_ref=dst, send_sem=send, recv_sem=recv,
+            device_id=(tile, peer_of(k)), device_id_type=MESH,
+        )
+        copy.start()
+        return copy
+
+    barrier = pltpu.get_barrier_semaphore()
+    for k in range(1, n_view):
+        pl.semaphore_signal(barrier, inc=1, device_id=(tile, peer_of(k)), device_id_type=MESH)
+    groups = cols // LANES
+    total_blocks = ratios_ref.shape[0]
+    bins = w_ref.shape[1]
+    size = lists_ref.shape[0] // 2
 
     def fill(step, carry):
         for u in range(UNROLL):
@@ -178,66 +225,33 @@
 
     lax.fori_loop(0, total_blocks // UNROLL, fill, 0)
     lhs[total_blocks] = jnp.zeros(lhs.shape[1:], jnp.bfloat16)
-    acc[...] = jnp.zeros_like(acc)
-    for w in range(views):
-        count = counts_ref[w]
-
-        def body(step, carry, w=w, count=count):
-            spread = []
-            for u in range(UNROLL):
-                k = step * UNROLL + u
-                block = cross_ref[w * 2 * slots + k] + w * blocks_view
-                at = jnp.where(k < count, block, total_blocks)
-                spread.append(
-                    jnp.dot(lhs[at], w_ref[w * slots + k], preferred_element_type=jnp.float32)
-                )
-            for u in range(UNROLL):
-                seg = cross_ref[w * 2 * slots + slots + step * UNROLL + u]
-                acc[seg] += spread[u]
-            return carry
-
-        lax.fori_loop(0, (count + UNROLL - 1) // UNROLL, body, 0)
-    for q in range(acc.shape[0]):
-        for c in range(chunks):
-            back_ref[c, q] = acc[q, c * pc : (c + 1) * pc].astype(jnp.bfloat16)
-        sens_ref[q : q + 1] = acc[q, planes : planes + 1]
-
-
-def update_kernel(
-    sizes, back_ref, sens_ref, vol_ref, halo_ref, out_ref, rback, rsens, natural,
-    send_sem, ssend_sem, srecv_sem, gsend_sem, recv_sem, grecv_sem,
-):
-    n_tile, n_view, seg_cols = sizes
-    tile = lax.axis_index("tile")
-    me = lax.axis_index("view")
-    planes, rows, cols = vol_ref.shape
-    pc = planes // n_view
-    per_group = LANES // seg_cols
-
-    def peer_of(k):
-        return lax.rem(me + k, n_view)
-
-    def push(src, dst, send, recv, k):
-        copy = pltpu.make_async_remote_copy(
-            src_ref=src, dst_ref=dst, send_sem=send, recv_sem=recv,
-            device_id=(tile, peer_of(k)), device_id_type=MESH,
-        )
-        copy.start()
-        return copy
-
-    barrier = pltpu.get_barrier_semaphore()
-    for k in range(1, n_view):
-        pl.semaphore_signal(barrier, inc=1, device_id=(tile, peer_of(k)), device_id_type=MESH)
-    pl.semaphore_wait(barrier, n_view - 1)
-    groups = cols // LANES
+
+    def project(q, carry):
+        total = jnp.zeros((lhs.shape[1], w_ref.shape[2]), jnp.float32)
+        for j in range(room):
+            total = total + jnp.dot(
+                lhs[lists_ref[size + q * room + j]],
+                w_ref[lists_ref[q * room + j]],
+                preferred_element_type=jnp.float32,
+            )
+        for c in range(n_view):
+            back_ref[c, q] = total[c * pc : (c + 1) * pc].astype(jnp.bfloat16)
+        sens_ref[pl.ds(q, 1)] = total[planes : planes + 1]
+        return carry
+
     order = sorted(range(1, n_view), key=lambda k: -min(k, n_view - k))
     rest = pl.ds(1, n_view - 1)
-    for k in order:
-        push(sens_ref, rsens.at[k], ssend_sem, srecv_sem, k)
     for g in range(groups):
+        lax.fori_loop(per_group * g, per_group * (g + 1), project, 0)
+        if g == 0:
+            pl.semaphore_wait(barrier, n_view - 1)
         piece = pl.ds(per_group * g, per_group)
         for k in order:
             push(back_ref.at[peer_of(k), piece], rback.at[k, piece], send_sem, recv_sem.at[g], k)
+        if g % 2 == 1:
+            part = pl.ds(per_group * (g - 1), 2 * per_group)
+            for k in order:
+                push(sens_ref.at[part], rsens.at[k, part], ssend_sem, srecv_sem.at[g // 2], k)
     first = pl.multiple_of(me * pc, pc)
     v = vol_ref[pl.ds(first, pc)]
     before = vol_ref[jnp.maximum(first - 1, 0)]
@@ -260,21 +274,31 @@
     penalty += term(jnp.where(col == cols - 1, 0.0, pltpu.roll(v, cols - 1, 2)))
     scale = v / (1.0 + penalty)
 
-    pltpu.make_async_copy(rsens.at[rest], rsens.at[rest], srecv_sem).wait()
-    sens = sens_ref[...]
-    for k in range(1, n_view):
-        sens = sens + rsens[k]
+    sens_of = {}
+
+    def sens_total(g):
+        if g not in sens_of:
+            part = pl.ds(per_group * g, 2 * per_group)
+            landed = rsens.at[rest, part]
+            pltpu.make_async_copy(landed, landed, srecv_sem.at[g // 2]).wait()
+            sens = sens_ref[part]
+            for k in range(1, n_view):
+                sens = sens + rsens[k, part]
+            sens_of[g] = sens
+        return sens_of[g]
 
     def finish(g):
         landed = rback.at[rest, pl.ds(per_group * g, per_group)]
         pltpu.make_async_copy(landed, landed, recv_sem.at[g]).wait()
+        sens = sens_total(g - g % 2)
         parts = []
         for j in range(per_group):
             q = per_group * g + j
             total = back_ref[me, q].astype(jnp.float32)
             for k in range(1, n_view):
                 total = total + rback[k, q].astype(jnp.float32)
-            parts.append(total / sens[q : q + 1])
+            at = per_group * (g % 2) + j
+            parts.append(total / sens[at : at + 1])
         for h in range(rows // per_group):
             lanes = slice(LANES * h, LANES * (h + 1))
             for i, out in enumerate(swap_chunks([x[:, lanes] for x in parts], seg_cols)):
@@ -347,18 +371,20 @@
     cross = crossings[0].transpose(0, 2, 1).reshape(views * 2 * slots)
     count = counts[0]
     slot_weights = weights.reshape(views * slots, bins, seg_pixels)
-    dense, edges = pl.pallas_call(
+    dense, edges, lists = pl.pallas_call(
         functools.partial(forward_kernel, dims),
         out_shape=(
             jax.ShapeDtypeStruct((total, half, LANES), bf16),
             jax.ShapeDtypeStruct((2, pc, cols), f32),
+            jax.ShapeDtypeStruct((2 * (seg_total * 2 * views + LANES),), jnp.int32),
         ),
         in_specs=[smem, smem, vmem, vmem],
-        out_specs=(vmem, vmem),
+        out_specs=(vmem, vmem, smem),
         scratch_shapes=[
             pltpu.VMEM((cols // LANES, planes * rows, LANES), f32),
             pltpu.VMEM((seg_total, 2 * planes, seg_pixels), bf16),
             pltpu.VMEM((total + 1, half, LANES), f32),
+            pltpu.SMEM((seg_total,), jnp.int32),
         ],
         compiler_params=local,
         name="forward",
@@ -378,35 +404,23 @@
         compiler_params=remote(1),
         name="exchange",
     )(dense, measured[0, 0, 0].T, edges)
-    back, sens = pl.pallas_call(
-        functools.partial(backward_kernel, dims),
-        out_shape=(
-            jax.ShapeDtypeStruct((n_view, seg_total, pc, seg_pixels), bf16),
-            jax.ShapeDtypeStruct((seg_total, seg_pixels), f32),
-        ),
-        in_specs=[smem, smem, vmem, vmem],
-        out_specs=(vmem, vmem),
+    return pl.pallas_call(
+        functools.partial(update_kernel, (n_tile, n_view, seg_cols, 2 * views)),
+        out_shape=jax.ShapeDtypeStruct((planes, rows, cols), f32),
+        in_specs=[smem, vmem, vmem, vmem, vmem],
+        out_specs=vmem,
         scratch_shapes=[
             pltpu.VMEM((total + 1, planes + 8, bins), bf16),
-            pltpu.VMEM((seg_total, planes + 8, seg_pixels), f32),
-        ],
-        compiler_params=local,
-        name="backward",
-    )(cross, count, ratios, slot_weights)
-    return pl.pallas_call(
-        functools.partial(update_kernel, (n_tile, n_view, seg_cols)),
-        out_shape=jax.ShapeDtypeStruct((planes, rows, cols), f32),
-        in_specs=[vmem, vmem, vmem, vmem],
-        out_specs=vmem,
-        scratch_shapes=[
+            pltpu.VMEM((n_view, seg_total, pc, seg_pixels), bf16),
+            pltpu.VMEM((seg_total, seg_pixels), f32),
             pltpu.VMEM((n_view, seg_total, pc, seg_pixels), bf16),
             pltpu.VMEM((n_view, seg_total, seg_pixels), f32),
             pltpu.VMEM((cols // LANES, pc * rows, LANES), f32),
         ]
-        + [dma, dma, dma, dma, dma((cols // LANES,)), dma((2, n_view // 2, cols // LANES))],
+        + [dma, dma, dma((cols // LANES // 2,)), dma, dma((cols // LANES,)), dma((2, n_view // 2, cols // LANES))],
         compiler_params=remote(2),
         name="update",
-    )(back, sens, volume, halo)
+    )(lists, ratios, slot_weights, volume, halo)
 
 
 def solution(mesh):

time: 92.6 us -> 88.4 us (0.955)
  Pallas kernels: 84.8 us -> 80.5 us
    pallas_call x1 -> x0, Pallas kernels: 6.51 us -> none  [per_device(): pl.pallas_call(functools.partial(backward_kernel, dims), out_shape=(jax.S...]
    pallas_call x1, Pallas kernels: 37.9 us -> 39.3 us  [per_device(): pl.pallas_call(functools.partial(update_kernel, (n_tile, n_view, seg_cols...]
where the time goes in v4:
time: 88.4 us; the launch traced here: 86.8 us
  Pallas kernels  80.5 us (91%)
  local copies, waits for them, and re-layouts  6.25 us (7%)
    pallas_call x1, Pallas kernels, per_device(): pl.pallas_call(functools.partial(update_kernel, (n_tile, n_view, seg_cols...  39.3 us
    pallas_call x1, Pallas kernels, per_device(): pl.pallas_call(functools.partial(exchange_kernel, n_tile), out_shape=(jax...  34.3 us
    pallas_call x1, Pallas kernels, per_device(): pl.pallas_call(functools.partial(forward_kernel, dims), out_shape=(jax.Sh...  6.88 us
    unnamed x13, local copies, waits for them, and re-layouts  5.48 us

profile of v4, /device:TPU:6, one launch (start us, length us, event | category | flops | bytes accessed | tf_op | source)
XLA Modules:
  0.0 86.8 jit_solution(13122581353822695639)
XLA Ops:
  0.0 0.8 reshape.9.cross_ref
  0.8 0.0 copy-start
  0.8 1.9 %copy-done = bf16[1,4,32,48,256]{4,3,2,1,0:T(8,128)(2,1)S(1)} copy-done((bf16[1,4,32,48,256]{4,3,2,1,0:T(8,128)(2,1)S(1)}, bf16[1,4,32,48,256]{4,3,2,1,0:T(8,128)(2,1)}, u32[]{:S(2)}) %copy-start) | copy-done | bytes 3145752
  2.7 0.0 copy-start.2
  2.7 1.2 %copy-done.2 = f32[64,8,512]{2,1,0:T(8,128)S(1)} copy-done((f32[64,8,512]{2,1,0:T(8,128)S(1)}, f32[64,8,512]{2,1,0:T(8,128)}, u32[]{:S(2)}) %copy-start.2) | copy-done | bytes 1048600
  3.9 0.0 copy-start.5
  3.9 0.7 copy-done.5
  4.5 0.0 copy-start.1
  4.5 0.0 copy-start.3
  4.5 6.9 %forward.1 = (bf16[64,24,128]{2,1,0:T(8,128)(2,1)S(1)}, f32[2,8,512]{2,1,0:T(8,128)S(1)}, s32[512]{0:T(512)S(1)}) custom-call(s32[256]{0:T(256)S(1)} %reshape.9.cross_ref, s32[4]{0:T(128)S(1)} %bitcast.13, f32[512,512]{1,0:T(8,128)S(1)} %bitcast.11, bf16[128,48,256]{2,1,0:T(8,128)(2,1)S(1)} %bitcast.9), custom_call_target="tpu_custom_call" | custom-call | tf_op jit(solution)/shard_map/forward/pallas_call | solution.py:374
  11.4 0.0 copy-start.4
  11.4 0.7 copy-done.4
  12.2 34.3 %exchange.1 = (bf16[64,24,128]{2,1,0:T(8,128)(2,1)S(1)}, f32[2,8,512]{2,1,0:T(8,128)S(1)}) custom-call(bf16[64,24,128]{2,1,0:T(8,128)(2,1)S(1)} %get-tuple-element.11.dense_ref, f32[48,64]{1,0:T(8,128)S(1)} %bitcast.12, f32[2,8,512]{2,1,0:T(8,128)S(1)} %get-tuple-element.12.edges_ref), custom_call_target="tpu_custom_call" | custom-call | tf_op jit(solution)/shard_map/exchange/pallas_call | solution.py:392
  46.5 0.0 copy-done.1
  46.5 0.0 copy-done.3
  46.5 39.3 %update.1 = f32[64,8,512]{2,1,0:T(8,128)S(1)} custom-call(s32[512]{0:T(512)S(1)} %get-tuple-element.10.lists_ref, bf16[64,24,128]{2,1,0:T(8,128)(2,1)S(1)} %get-tuple-element.13.ratios_ref, bf16[128,48,256]{2,1,0:T(8,128)(2,1)S(1)} %bitcast.10, f32[64,8,512]{2,1,0:T(8,128)S(1)} %copy-done.3, f32[2,8,512]{2,1,0:T(8,128)S(1)} %get-tuple-element.14.halo_ref), custom_call_target="tpu_custom_call" | custom-call | tf_op jit(solution)/shard_map/update/pallas_call | solution.py:407
  85.8 1.0 %copy.7 = f32[64,8,512]{2,1,0:T(8,128)} copy(f32[64,8,512]{2,1,0:T(8,128)S(1)} %update.1) | data formatting | bytes 2097152
Async XLA Ops:
  0.8 1.9 %copy-start = (bf16[1,4,32,48,256]{4,3,2,1,0:T(8,128)(2,1)S(1)}, bf16[1,4,32,48,256]{4,3,2,1,0:T(8,128)(2,1)}, u32[]{:S(2)}) copy-start(bf16[1,4,32,48,256]{4,3,2,1,0:T(8,128)(2,1)} %param.6) | copy-start | bytes 9437188
  2.7 1.2 %copy-start.2 = (f32[64,8,512]{2,1,0:T(8,128)S(1)}, f32[64,8,512]{2,1,0:T(8,128)}, u32[]{:S(2)}) copy-start(f32[64,8,512]{2,1,0:T(8,128)} %vol_ref.1) | copy-start | bytes 3145732
  3.9 0.7 copy-start.5
  4.5 41.9 %copy-start.1 = (bf16[1,4,32,48,256]{4,3,2,1,0:T(8,128)(2,1)S(1)}, bf16[1,4,32,48,256]{4,3,2,1,0:T(8,128)(2,1)}, u32[]{:S(2)}) copy-start(bf16[1,4,32,48,256]{4,3,2,1,0:T(8,128)(2,1)} %param.6) | copy-start | bytes 9437188
  4.5 41.9 %copy-start.3 = (f32[64,8,512]{2,1,0:T(8,128)S(1)}, f32[64,8,512]{2,1,0:T(8,128)}, u32[]{:S(2)}) copy-start(f32[64,8,512]{2,1,0:T(8,128)} %vol_ref.1) | copy-start | bytes 3145732
  11.4 0.7 copy-start.4

commit v5 on v4

--- a/solution.py
+++ b/solution.py
@@ -117,6 +117,9 @@
     def peer_of(k):
         return lax.rem(me + k, n_tile)
 
+    def offset(i):
+        return n_tile // 2 + (i + 1) // 2 * (2 * (i % 2) - 1)
+
     barrier = pltpu.get_barrier_semaphore()
 
     def greet(k, carry):
@@ -126,7 +129,8 @@
     lax.fori_loop(1, n_tile, greet, 0)
     pl.semaphore_wait(barrier, n_tile - 1)
 
-    def send(k, carry):
+    def send(i, carry):
+        k = offset(i)
         peer = peer_of(k)
         pltpu.make_async_remote_copy(
             src_ref=dense_ref.at[peer],
@@ -138,7 +142,7 @@
         ).start()
         return carry
 
-    lax.fori_loop(1, n_tile, send, 0)
+    lax.fori_loop(0, n_tile - 1, send, 0)
     halos = []
     for side, step in ((0, 1), (1, n_tile - 1)):
         halos.append(
@@ -164,7 +168,8 @@
     ratio = (counted / (total + BACKGROUND)).astype(jnp.bfloat16)
     ratios_ref[me] = ratio
 
-    def spread(k, carry):
+    def spread(i, carry):
+        k = offset(i)
         pltpu.make_async_remote_copy(
             src_ref=ratios_ref.at[me],
             dst_ref=ratios_ref.at[me],
@@ -175,7 +180,7 @@
         ).start()
         return carry
 
-    lax.fori_loop(1, n_tile, spread, 0)
+    lax.fori_loop(0, n_tile - 1, spread, 0)
     pltpu.make_async_copy(recv.at[rest], recv.at[rest], grecv_sem).wait()
     pltpu.make_async_copy(recv.at[rest], recv.at[rest], send_sem).wait()
     pltpu.make_async_copy(recv.at[rest], recv.at[rest], gsend_sem).wait()

time: 88.4 us -> 88.7 us (level)
  the two profiles are of different devices: /device:TPU:6 before, /device:TPU:64 now
where the time goes in v5:
time: 88.7 us; the launch traced here: 88.4 us
  Pallas kernels  82.1 us (93%)
  local copies, waits for them, and re-layouts  6.25 us (7%)
    pallas_call x1, Pallas kernels, per_device(): pl.pallas_call(functools.partial(update_kernel, (n_tile, n_view, seg_cols...  41.9 us
    pallas_call x1, Pallas kernels, per_device(): pl.pallas_call(functools.partial(exchange_kernel, n_tile), out_shape=(jax...  33.3 us
    pallas_call x1, Pallas kernels, per_device(): pl.pallas_call(functools.partial(forward_kernel, dims), out_shape=(jax.Sh...  6.89 us
    unnamed x13, local copies, waits for them, and re-layouts  5.48 us

profile of v5, /device:TPU:64, one launch (start us, length us, event | category | flops | bytes accessed | tf_op | source)
XLA Modules:
  0.0 88.4 jit_solution(8195202500443257976)
XLA Ops:
  0.0 0.8 reshape.9.cross_ref
  0.8 0.0 copy-start
  0.8 1.9 %copy-done = bf16[1,4,32,48,256]{4,3,2,1,0:T(8,128)(2,1)S(1)} copy-done((bf16[1,4,32,48,256]{4,3,2,1,0:T(8,128)(2,1)S(1)}, bf16[1,4,32,48,256]{4,3,2,1,0:T(8,128)(2,1)}, u32[]{:S(2)}) %copy-start) | copy-done | bytes 3145752
  2.7 0.0 copy-start.2
  2.7 1.2 %copy-done.2 = f32[64,8,512]{2,1,0:T(8,128)S(1)} copy-done((f32[64,8,512]{2,1,0:T(8,128)S(1)}, f32[64,8,512]{2,1,0:T(8,128)}, u32[]{:S(2)}) %copy-start.2) | copy-done | bytes 1048600
  3.9 0.0 copy-start.5
  3.9 0.7 copy-done.5
  4.5 0.0 copy-start.1
  4.5 0.0 copy-start.3
  4.5 6.9 %forward.1 = (bf16[64,24,128]{2,1,0:T(8,128)(2,1)S(1)}, f32[2,8,512]{2,1,0:T(8,128)S(1)}, s32[512]{0:T(512)S(1)}) custom-call(s32[256]{0:T(256)S(1)} %reshape.9.cross_ref, s32[4]{0:T(128)S(1)} %bitcast.13, f32[512,512]{1,0:T(8,128)S(1)} %bitcast.11, bf16[128,48,256]{2,1,0:T(8,128)(2,1)S(1)} %bitcast.9), custom_call_target="tpu_custom_call" | custom-call | tf_op jit(solution)/shard_map/forward/pallas_call | solution.py:379
  11.4 0.0 copy-start.4
  11.5 0.7 copy-done.4
  12.2 33.3 %exchange.1 = (bf16[64,24,128]{2,1,0:T(8,128)(2,1)S(1)}, f32[2,8,512]{2,1,0:T(8,128)S(1)}) custom-call(bf16[64,24,128]{2,1,0:T(8,128)(2,1)S(1)} %get-tuple-element.11.dense_ref, f32[48,64]{1,0:T(8,128)S(1)} %bitcast.12, f32[2,8,512]{2,1,0:T(8,128)S(1)} %get-tuple-element.12.edges_ref), custom_call_target="tpu_custom_call" | custom-call | tf_op jit(solution)/shard_map/exchange/pallas_call | solution.py:397
  45.4 0.0 copy-done.1
  45.5 0.0 copy-done.3
  45.5 41.9 %update.1 = f32[64,8,512]{2,1,0:T(8,128)S(1)} custom-call(s32[512]{0:T(512)S(1)} %get-tuple-element.10.lists_ref, bf16[64,24,128]{2,1,0:T(8,128)(2,1)S(1)} %get-tuple-element.13.ratios_ref, bf16[128,48,256]{2,1,0:T(8,128)(2,1)S(1)} %bitcast.10, f32[64,8,512]{2,1,0:T(8,128)S(1)} %copy-done.3, f32[2,8,512]{2,1,0:T(8,128)S(1)} %get-tuple-element.14.halo_ref), custom_call_target="tpu_custom_call" | custom-call | tf_op jit(solution)/shard_map/update/pallas_call | solution.py:412
  87.4 1.0 %copy.7 = f32[64,8,512]{2,1,0:T(8,128)} copy(f32[64,8,512]{2,1,0:T(8,128)S(1)} %update.1) | data formatting | bytes 2097152
Async XLA Ops:
  0.8 1.9 %copy-start = (bf16[1,4,32,48,256]{4,3,2,1,0:T(8,128)(2,1)S(1)}, bf16[1,4,32,48,256]{4,3,2,1,0:T(8,128)(2,1)}, u32[]{:S(2)}) copy-start(bf16[1,4,32,48,256]{4,3,2,1,0:T(8,128)(2,1)} %param.6) | copy-start | bytes 9437188
  2.7 1.2 %copy-start.2 = (f32[64,8,512]{2,1,0:T(8,128)S(1)}, f32[64,8,512]{2,1,0:T(8,128)}, u32[]{:S(2)}) copy-start(f32[64,8,512]{2,1,0:T(8,128)} %vol_ref.1) | copy-start | bytes 3145732
  3.9 0.7 copy-start.5
  4.5 40.9 %copy-start.1 = (bf16[1,4,32,48,256]{4,3,2,1,0:T(8,128)(2,1)S(1)}, bf16[1,4,32,48,256]{4,3,2,1,0:T(8,128)(2,1)}, u32[]{:S(2)}) copy-start(bf16[1,4,32,48,256]{4,3,2,1,0:T(8,128)(2,1)} %param.6) | copy-start | bytes 9437188
  4.5 40.9 %copy-start.3 = (f32[64,8,512]{2,1,0:T(8,128)S(1)}, f32[64,8,512]{2,1,0:T(8,128)}, u32[]{:S(2)}) copy-start(f32[64,8,512]{2,1,0:T(8,128)} %vol_ref.1) | copy-start | bytes 3145732
  11.4 0.7 copy-start.4

commit v6 on v4

--- a/solution.py
+++ b/solution.py
@@ -34,7 +34,8 @@
 
 
 def forward_kernel(
-    dims, cross_ref, counts_ref, vol_ref, w_ref, dense_ref, edges_ref, lists_ref, vol, segs, acc, used
+    dims, cross_ref, counts_ref, vol_ref, w_ref, dense_ref, edges_ref, lists_ref,
+    sens_ref, vol, segs, acc, used, sums,
 ):
     planes, rows, cols, seg_cols, views, slots, blocks_view, bins, pc = dims
     per_group = LANES // seg_cols
@@ -71,6 +72,7 @@
                 segs[per_group * g + j, 0:planes, lanes] = out
                 segs[per_group * g + j, planes : 2 * planes, lanes] = out
     acc[...] = jnp.zeros_like(acc)
+    sums[...] = jnp.zeros_like(sums)
     low = lax.broadcasted_iota(jnp.int32, (half, LANES), 1) < planes
 
     for w in range(views):
@@ -99,15 +101,18 @@
                 place = jnp.where(k < count, seg * room + place, seg_total * room)
                 lists_ref[place] = w * slots + k
                 lists_ref[size + place] = block
+                tall = w_ref[w * slots + k].astype(jnp.float32).reshape(bins // 8, 8, -1)
+                sums[jnp.where(k < count, seg, seg_total)] += jnp.sum(tall, axis=0)
             return carry
 
         lax.fori_loop(0, (count + UNROLL - 1) // UNROLL, body, 0)
     dense_ref[...] = acc[0:total_blocks].astype(jnp.bfloat16)
+    sens_ref[...] = jnp.sum(sums[0:seg_total], axis=1)
 
 
 def exchange_kernel(
-    n_tile, dense_ref, meas_ref, edges_ref, ratios_ref, halo_ref, recv,
-    send_sem, recv_sem, gsend_sem, grecv_sem, hsend_sem, hrecv_sem,
+    n_tile, n_view, dense_ref, meas_ref, edges_ref, sens_ref, ratios_ref, halo_ref, rsens_ref, recv,
+    send_sem, recv_sem, gsend_sem, grecv_sem, ssend_sem, srecv_sem, hsend_sem, hrecv_sem,
 ):
     me = lax.axis_index("tile")
     view = lax.axis_index("view")
@@ -124,7 +129,11 @@
         return carry
 
     lax.fori_loop(1, n_tile, greet, 0)
-    pl.semaphore_wait(barrier, n_tile - 1)
+    for k in range(1, n_view):
+        above = lax.rem(view + k, n_view)
+        pl.semaphore_signal(barrier, inc=1, device_id=(me, above), device_id_type=MESH)
+    rsens_ref[0] = sens_ref[...]
+    pl.semaphore_wait(barrier, n_tile + n_view - 2)
 
     def send(k, carry):
         peer = peer_of(k)
@@ -139,6 +148,15 @@
         return carry
 
     lax.fori_loop(1, n_tile, send, 0)
+    for k in range(1, n_view):
+        pltpu.make_async_remote_copy(
+            src_ref=sens_ref,
+            dst_ref=rsens_ref.at[k],
+            send_sem=ssend_sem,
+            recv_sem=srecv_sem,
+            device_id=(me, lax.rem(view + k, n_view)),
+            device_id_type=MESH,
+        ).start()
     halos = []
     for side, step in ((0, 1), (1, n_tile - 1)):
         halos.append(
@@ -181,12 +199,15 @@
     pltpu.make_async_copy(recv.at[rest], recv.at[rest], gsend_sem).wait()
     for copy in halos:
         copy.wait()
+    others = rsens_ref.at[pl.ds(1, n_view - 1)]
+    pltpu.make_async_copy(others, others, srecv_sem).wait()
+    pltpu.make_async_copy(others, others, ssend_sem).wait()
 
 
 def update_kernel(
-    sizes, lists_ref, ratios_ref, w_ref, vol_ref, halo_ref, out_ref,
-    lhs, back_ref, sens_ref, rback, rsens, natural,
-    send_sem, ssend_sem, srecv_sem, gsend_sem, recv_sem, grecv_sem,
+    sizes, lists_ref, ratios_ref, w_ref, vol_ref, halo_ref, rsens, out_ref,
+    lhs, back_ref, rback, natural,
+    send_sem, gsend_sem, recv_sem, grecv_sem,
 ):
     n_tile, n_view, seg_cols, room = sizes
     tile = lax.axis_index("tile")
@@ -211,7 +232,6 @@
         pl.semaphore_signal(barrier, inc=1, device_id=(tile, peer_of(k)), device_id_type=MESH)
     groups = cols // LANES
     total_blocks = ratios_ref.shape[0]
-    bins = w_ref.shape[1]
     size = lists_ref.shape[0] // 2
 
     def fill(step, carry):
@@ -219,8 +239,7 @@
             b = step * UNROLL + u
             x = ratios_ref[b].astype(jnp.float32)
             x = jnp.concatenate([x, pltpu.roll(x, planes, 1)], axis=0)
-            lhs[b, 0:planes] = jnp.transpose(x)[0:planes].astype(jnp.bfloat16)
-            lhs[b, planes:] = jnp.ones((lhs.shape[1] - planes, bins), jnp.bfloat16)
+            lhs[b] = jnp.transpose(x)[0:planes].astype(jnp.bfloat16)
         return carry
 
     lax.fori_loop(0, total_blocks // UNROLL, fill, 0)
@@ -236,7 +255,6 @@
             )
         for c in range(n_view):
             back_ref[c, q] = total[c * pc : (c + 1) * pc].astype(jnp.bfloat16)
-        sens_ref[pl.ds(q, 1)] = total[planes : planes + 1]
         return carry
 
     order = sorted(range(1, n_view), key=lambda k: -min(k, n_view - k))
@@ -248,10 +266,6 @@
         piece = pl.ds(per_group * g, per_group)
         for k in order:
             push(back_ref.at[peer_of(k), piece], rback.at[k, piece], send_sem, recv_sem.at[g], k)
-        if g % 2 == 1:
-            part = pl.ds(per_group * (g - 1), 2 * per_group)
-            for k in order:
-                push(sens_ref.at[part], rsens.at[k, part], ssend_sem, srecv_sem.at[g // 2], k)
     first = pl.multiple_of(me * pc, pc)
     v = vol_ref[pl.ds(first, pc)]
     before = vol_ref[jnp.maximum(first - 1, 0)]
@@ -274,31 +288,20 @@
     penalty += term(jnp.where(col == cols - 1, 0.0, pltpu.roll(v, cols - 1, 2)))
     scale = v / (1.0 + penalty)
 
-    sens_of = {}
-
-    def sens_total(g):
-        if g not in sens_of:
-            part = pl.ds(per_group * g, 2 * per_group)
-            landed = rsens.at[rest, part]
-            pltpu.make_async_copy(landed, landed, srecv_sem.at[g // 2]).wait()
-            sens = sens_ref[part]
-            for k in range(1, n_view):
-                sens = sens + rsens[k, part]
-            sens_of[g] = sens
-        return sens_of[g]
+    sens = rsens[0]
+    for k in range(1, n_view):
+        sens = sens + rsens[k]
 
     def finish(g):
         landed = rback.at[rest, pl.ds(per_group * g, per_group)]
         pltpu.make_async_copy(landed, landed, recv_sem.at[g]).wait()
-        sens = sens_total(g - g % 2)
         parts = []
         for j in range(per_group):
             q = per_group * g + j
             total = back_ref[me, q].astype(jnp.float32)
             for k in range(1, n_view):
                 total = total + rback[k, q].astype(jnp.float32)
-            at = per_group * (g % 2) + j
-            parts.append(total / sens[at : at + 1])
+            parts.append(total / sens[q : q + 1])
         for h in range(rows // per_group):
             lanes = slice(LANES * h, LANES * (h + 1))
             for i, out in enumerate(swap_chunks([x[:, lanes] for x in parts], seg_cols)):
@@ -338,7 +341,6 @@
                     if hop < reach(side, g):
                         relay(side, hop, g)
     for sent, sem in (
-        (rsens.at[rest], ssend_sem),
         (rback.at[rest], send_sem),
         (out_ref.at[pl.ds(0, planes - pc)], gsend_sem),
     ):
@@ -371,56 +373,57 @@
     cross = crossings[0].transpose(0, 2, 1).reshape(views * 2 * slots)
     count = counts[0]
     slot_weights = weights.reshape(views * slots, bins, seg_pixels)
-    dense, edges, lists = pl.pallas_call(
+    dense, edges, lists, sens = pl.pallas_call(
         functools.partial(forward_kernel, dims),
         out_shape=(
             jax.ShapeDtypeStruct((total, half, LANES), bf16),
             jax.ShapeDtypeStruct((2, pc, cols), f32),
             jax.ShapeDtypeStruct((2 * (seg_total * 2 * views + LANES),), jnp.int32),
+            jax.ShapeDtypeStruct((seg_total, seg_pixels), f32),
         ),
         in_specs=[smem, smem, vmem, vmem],
-        out_specs=(vmem, vmem, smem),
+        out_specs=(vmem, vmem, smem, vmem),
         scratch_shapes=[
             pltpu.VMEM((cols // LANES, planes * rows, LANES), f32),
             pltpu.VMEM((seg_total, 2 * planes, seg_pixels), bf16),
             pltpu.VMEM((total + 1, half, LANES), f32),
             pltpu.SMEM((seg_total,), jnp.int32),
+            pltpu.VMEM((seg_total + 1, 8, seg_pixels), f32),
         ],
         compiler_params=local,
         name="forward",
     )(cross, count, volume.reshape(planes * rows, cols), slot_weights)
-    ratios, halo = pl.pallas_call(
-        functools.partial(exchange_kernel, n_tile),
+    ratios, halo, rsens = pl.pallas_call(
+        functools.partial(exchange_kernel, n_tile, n_view),
         out_shape=(
             jax.ShapeDtypeStruct((total, half, LANES), bf16),
             jax.ShapeDtypeStruct((2, pc, cols), f32),
+            jax.ShapeDtypeStruct((n_view, seg_total, seg_pixels), f32),
         ),
-        in_specs=[vmem, vmem, vmem],
-        out_specs=(vmem, vmem),
+        in_specs=[vmem, vmem, vmem, vmem],
+        out_specs=(vmem, vmem, vmem),
         scratch_shapes=[
             pltpu.VMEM((n_tile, half, LANES), bf16),
-            dma, dma, dma, dma, dma((2,)), dma((2,)),
+            dma, dma, dma, dma, dma, dma, dma((2,)), dma((2,)),
         ],
         compiler_params=remote(1),
         name="exchange",
-    )(dense, measured[0, 0, 0].T, edges)
+    )(dense, measured[0, 0, 0].T, edges, sens)
     return pl.pallas_call(
         functools.partial(update_kernel, (n_tile, n_view, seg_cols, 2 * views)),
         out_shape=jax.ShapeDtypeStruct((planes, rows, cols), f32),
-        in_specs=[smem, vmem, vmem, vmem, vmem],
+        in_specs=[smem, vmem, vmem, vmem, vmem, vmem],
         out_specs=vmem,
         scratch_shapes=[
-            pltpu.VMEM((total + 1, planes + 8, bins), bf16),
+            pltpu.VMEM((total + 1, planes, bins), bf16),
             pltpu.VMEM((n_view, seg_total, pc, seg_pixels), bf16),
-            pltpu.VMEM((seg_total, seg_pixels), f32),
             pltpu.VMEM((n_view, seg_total, pc, seg_pixels), bf16),
-            pltpu.VMEM((n_view, seg_total, seg_pixels), f32),
             pltpu.VMEM((cols // LANES, pc * rows, LANES), f32),
         ]
-        + [dma, dma, dma((cols // LANES // 2,)), dma, dma((cols // LANES,)), dma((2, n_view // 2, cols // LANES))],
+        + [dma, dma, dma((cols // LANES,)), dma((2, n_view // 2, cols // LANES))],
         compiler_params=remote(2),
         name="update",
-    )(lists, ratios, slot_weights, volume, halo)
+    )(lists, ratios, slot_weights, volume, halo, rsens)
 
 
 def solution(mesh):

time: 88.4 us -> 85.2 us (0.964)
  the two profiles are of different devices: /device:TPU:6 before, /device:TPU:2 now
where the time goes in v6:
time: 85.2 us; the launch traced here: 84.2 us
  Pallas kernels  77.9 us (91%)
  local copies, waits for them, and re-layouts  6.25 us (7%)
    pallas_call x1, Pallas kernels, per_device(): pl.pallas_call(functools.partial(exchange_kernel, n_tile, n_view), out_sh...  35.8 us
    pallas_call x1, Pallas kernels, per_device(): pl.pallas_call(functools.partial(update_kernel, (n_tile, n_view, seg_cols...  35.1 us
    pallas_call x1, Pallas kernels, per_device(): pl.pallas_call(functools.partial(forward_kernel, dims), out_shape=(jax.Sh...  6.91 us
    unnamed x13, local copies, waits for them, and re-layouts  5.48 us

profile of v6, /device:TPU:2, one launch (start us, length us, event | category | flops | bytes accessed | tf_op | source)
XLA Modules:
  0.0 84.2 jit_solution(16209416256994316483)
XLA Ops:
  0.0 0.8 reshape.9.cross_ref
  0.8 0.0 copy-start
  0.8 1.9 %copy-done = bf16[1,4,32,48,256]{4,3,2,1,0:T(8,128)(2,1)S(1)} copy-done((bf16[1,4,32,48,256]{4,3,2,1,0:T(8,128)(2,1)S(1)}, bf16[1,4,32,48,256]{4,3,2,1,0:T(8,128)(2,1)}, u32[]{:S(2)}) %copy-start) | copy-done | bytes 3145752
  2.7 0.0 copy-start.2
  2.7 1.2 %copy-done.2 = f32[64,8,512]{2,1,0:T(8,128)S(1)} copy-done((f32[64,8,512]{2,1,0:T(8,128)S(1)}, f32[64,8,512]{2,1,0:T(8,128)}, u32[]{:S(2)}) %copy-start.2) | copy-done | bytes 1048600
  3.9 0.0 copy-start.5
  3.9 0.7 copy-done.5
  4.5 0.0 copy-start.1
  4.5 0.0 copy-start.3
  4.5 6.9 %forward.1 = (bf16[64,24,128]{2,1,0:T(8,128)(2,1)S(1)}, f32[2,8,512]{2,1,0:T(8,128)S(1)}, s32[512]{0:T(512)S(1)}, f32[16,256]{1,0:T(8,128)S(1)}) custom-call(s32[256]{0:T(256)S(1)} %reshape.9.cross_ref, s32[4]{0:T(128)S(1)} %bitcast.13, f32[512,512]{1,0:T(8,128)S(1)} %bitcast.11, bf16[128,48,256]{2,1,0:T(8,128)(2,1)S(1)} %bitcast.9), custom_call_target="tpu_custom_call" | custom-call | tf_op jit(solution)/shard_map/forward/pallas_call | solution.py:376
  11.5 0.0 copy-start.4
  11.5 0.7 copy-done.4
  12.2 35.8 %exchange.1 = (bf16[64,24,128]{2,1,0:T(8,128)(2,1)S(1)}, f32[2,8,512]{2,1,0:T(8,128)S(1)}, f32[8,16,256]{2,1,0:T(8,128)S(1)}) custom-call(bf16[64,24,128]{2,1,0:T(8,128)(2,1)S(1)} %get-tuple-element.13.dense_ref, f32[48,64]{1,0:T(8,128)S(1)} %bitcast.12, f32[2,8,512]{2,1,0:T(8,128)S(1)} %get-tuple-element.14.edges_ref, f32[16,256]{1,0:T(8,128)S(1)} %get-tuple-element.15.sens_ref), custom_call_target="tpu_custom_call" | custom-call | tf_op jit(solution)/shard_map/exchange/pallas_call | solution.py:396
  48.1 0.0 copy-done.1
  48.1 0.0 copy-done.3
  48.1 35.1 %update.1 = f32[64,8,512]{2,1,0:T(8,128)S(1)} custom-call(s32[512]{0:T(512)S(1)} %get-tuple-element.12.lists_ref, bf16[64,24,128]{2,1,0:T(8,128)(2,1)S(1)} %get-tuple-element.16.ratios_ref, bf16[128,48,256]{2,1,0:T(8,128)(2,1)S(1)} %bitcast.10, f32[64,8,512]{2,1,0:T(8,128)S(1)} %copy-done.3, f32[2,8,512]{2,1,0:T(8,128)S(1)} %get-tuple-element.17.halo_ref, ...), custom_call_target="tpu_custom_call" | custom-call | tf_op jit(solution)/shard_map/update/pallas_call | solution.py:412
  83.2 1.0 %copy.7 = f32[64,8,512]{2,1,0:T(8,128)} copy(f32[64,8,512]{2,1,0:T(8,128)S(1)} %update.1) | data formatting | bytes 2097152
Async XLA Ops:
  0.8 1.9 %copy-start = (bf16[1,4,32,48,256]{4,3,2,1,0:T(8,128)(2,1)S(1)}, bf16[1,4,32,48,256]{4,3,2,1,0:T(8,128)(2,1)}, u32[]{:S(2)}) copy-start(bf16[1,4,32,48,256]{4,3,2,1,0:T(8,128)(2,1)} %param.6) | copy-start | bytes 9437188
  2.7 1.2 %copy-start.2 = (f32[64,8,512]{2,1,0:T(8,128)S(1)}, f32[64,8,512]{2,1,0:T(8,128)}, u32[]{:S(2)}) copy-start(f32[64,8,512]{2,1,0:T(8,128)} %vol_ref.1) | copy-start | bytes 3145732
  3.9 0.7 copy-start.5
  4.5 43.5 %copy-start.1 = (bf16[1,4,32,48,256]{4,3,2,1,0:T(8,128)(2,1)S(1)}, bf16[1,4,32,48,256]{4,3,2,1,0:T(8,128)(2,1)}, u32[]{:S(2)}) copy-start(bf16[1,4,32,48,256]{4,3,2,1,0:T(8,128)(2,1)} %param.6) | copy-start | bytes 9437188
  4.5 43.5 %copy-start.3 = (f32[64,8,512]{2,1,0:T(8,128)S(1)}, f32[64,8,512]{2,1,0:T(8,128)}, u32[]{:S(2)}) copy-start(f32[64,8,512]{2,1,0:T(8,128)} %vol_ref.1) | copy-start | bytes 3145732
  11.5 0.7 copy-start.4
